TPU v7x, 128 devices: a whole 4x4x4 slice. The times are simulated.
128 devices in a mesh: ctx: 32 (over x, y, core), tp: 4 (over z).
Axes of the slice: x: 4, y: 4, z: 4, core: 2. Of those that a mesh axis runs over, the one named last changes fastest.
Arguments:
- queries: bfloat16 [512, 8192], P('ctx', 'tp'), may hold values from -60 to 60
- rotated_keys: bfloat16 [4096, 1024], P('ctx', 'tp'), may hold values from -7 to 7
- value_rows: bfloat16 [4096, 1024], P('ctx', 'tp'), may hold values from -6 to 6
- span_order: int32 [64], replicated, may hold values from 0 to 63, each once
- targets: int32 [512], replicated, may hold values from 0 to 65535
- out_weight: bfloat16 [8192, 4, 32, 64], P('tp', None, 'ctx'), may hold values from -0.0625 to 0.0625
- residual: bfloat16 [512, 4, 32, 64], P(None, 'tp', 'ctx'), may hold values from -3 to 3
- norm_gain: float32 [4, 32, 64], P('tp', 'ctx'), may hold values from 0.5 to 1.5
- head_weight: bfloat16 [8192, 65536], P('tp', 'ctx'), may hold values from -2.253903 to 2.253903
Outputs:
- loss: float32 [], replicated
- grad_normed: bfloat16 [512, 8192], P('ctx', 'tp')
- grad_head: bfloat16 [8192, 65536], P('tp', 'ctx')
Inputs may be any that keep to these rules, and one draw needn't show every extreme that they name: `span_order`: each span number appears once.
All inputs are finite; a program needn't handle non-finite values.
Results may differ from a plain program's by a relative error of at most 0.012.
Values may be sent and summed in bfloat16 or wider, within the bound.
No kernel may reach another device: no remote copies, remote signals or barrier semaphores. Data moves between devices by JAX's collectives and lax.ppermute only.
A program may use at most 128 MiB of HBM per device.

v0:
```python
import jax
import jax.numpy as jnp
from jax import lax
from jax.sharding import PartitionSpec as P

D = 8192
QUERY_HEADS = 64
KEY_VALUE_HEADS = 8
HEAD_SIZE = 128


EPSILON = 1e-05
MASKED = -1e30


def slot_positions(span_order, total_rows, slot_rows, span_rows, first_row):
    slots = jnp.arange(total_rows, dtype=jnp.int32)
    owners = slots // slot_rows
    table = owners[:, None] == jnp.arange(span_order.shape[0], dtype=jnp.int32)[None, :]
    starts = jnp.sum(jnp.where(table, span_order[None, :], 0), axis=1)
    return starts * span_rows + first_row + slots % slot_rows


def head_scores(grouped_queries, piece_keys):
    divided_keys = piece_keys.reshape(piece_keys.shape[0], -1, HEAD_SIZE)
    return jnp.einsum(
        "tkgd,skd->kgts", grouped_queries, divided_keys, preferred_element_type=jnp.float32
    ) * HEAD_SIZE ** (-0.5)


def score_stats(grouped_queries, mine, positions):

    def score_update(carry, piece, offset):
        visible = positions[None, :] <= mine[:, None]

        def score_accumulate(state):
            scores = jnp.where(visible, head_scores(grouped_queries, piece), MASKED)
            fresh = jnp.maximum(state[0], jnp.max(scores, axis=-1))
            added = jnp.sum(jnp.where(visible, jnp.exp(scores - fresh[..., None]), 0.0), axis=-1)
            return (fresh, added)

        return lax.cond(jnp.any(visible), score_accumulate, lambda state: state, carry)

    return score_update


def weighted_values(grouped_queries, mine, positions, peak, totals):

    def weighted_update(carry, pieces, offset):
        piece_keys, piece_values = pieces
        visible = positions[None, :] <= mine[:, None]

        def weighted_accumulate(state):
            scores = jnp.where(visible, head_scores(grouped_queries, piece_keys), MASKED)
            weights = jnp.where(visible, jnp.exp(scores - peak[..., None]), 0.0) / totals[..., None]
            divided_values = piece_values.reshape(piece_values.shape[0], -1, HEAD_SIZE)
            return jnp.einsum(
                "kgts,skd->tkgd",
                weights.astype(jnp.bfloat16),
                divided_values,
                preferred_element_type=jnp.float32,
            )

        return lax.cond(jnp.any(visible), weighted_accumulate, lambda state: state, carry)

    return weighted_update


def per_device(
    queries,
    rotated_keys,
    value_rows,
    span_order,
    targets,
    out_weight,
    residual,
    norm_gain,
    head_weight,
):
    tok_dev = rotated_keys.shape[0]
    q_dev = queries.shape[0]
    span_rows = tok_dev // 2
    q_span = q_dev // 2
    total_keys = tok_dev * lax.axis_size("ctx")
    total_rows = q_dev * lax.axis_size("ctx")
    positions = slot_positions(span_order, total_keys, span_rows, span_rows, 0)
    query_pos = slot_positions(span_order, total_rows, q_span, span_rows, span_rows - q_span)
    mine = lax.dynamic_slice_in_dim(query_pos, lax.axis_index("ctx") * q_dev, q_dev)
    group_size = QUERY_HEADS // KEY_VALUE_HEADS
    local_kv = rotated_keys.shape[1] // HEAD_SIZE
    grouped_queries = queries.reshape(q_dev, local_kv, group_size, HEAD_SIZE)
    start_stats = (
        jnp.full((local_kv, group_size, q_dev), MASKED, jnp.float32),
        jnp.zeros((local_kv, group_size, q_dev), jnp.float32),
    )
    start_acc = jnp.zeros((q_dev, local_kv, group_size, HEAD_SIZE), jnp.float32)
    stats_step = score_stats(grouped_queries, mine, positions)
    all_keys, all_values = (
        lax.all_gather(rotated_keys, "ctx", axis=0, tiled=True),
        lax.all_gather(value_rows, "ctx", axis=0, tiled=True),
    )
    peak, totals = stats_step(start_stats, all_keys, 0)
    value_step = weighted_values(grouped_queries, mine, positions, peak, totals)
    attn_acc = value_step(start_acc, (all_keys, all_values), 0)
    attn = attn_acc.astype(jnp.bfloat16).reshape(q_dev, -1)
    slice_width = out_weight.shape[3]
    out_local = out_weight.reshape(out_weight.shape[0], -1)
    mixed = jnp.dot(
        lax.all_gather(attn, "ctx", axis=0, tiled=True),
        out_local,
        preferred_element_type=jnp.float32,
    )
    mixed = lax.psum_scatter(
        mixed.reshape(total_rows, -1, slice_width), "tp", scatter_dimension=1, tiled=True
    )
    hidden = residual.reshape(total_rows, slice_width).astype(jnp.float32) + mixed.reshape(
        total_rows, slice_width
    )
    squares = lax.psum(jnp.sum(hidden * hidden, axis=1), ("ctx", "tp"))
    normed = (
        hidden * lax.rsqrt(squares / D + EPSILON)[:, None] * norm_gain.reshape(1, slice_width)
    ).astype(jnp.bfloat16)
    block = lax.all_gather(normed, "ctx", axis=1, tiled=True)
    vocab_width = head_weight.shape[1]
    first_col = lax.axis_index("ctx") * vocab_width
    logits = lax.psum(jnp.dot(block, head_weight, preferred_element_type=jnp.float32), "tp")
    columns = jnp.arange(vocab_width, dtype=jnp.int32)[None, :] + first_col
    target_hit = columns == targets[:, None]
    local_peak = jnp.max(logits, axis=1)
    picked = jnp.sum(jnp.where(target_hit, logits, 0.0), axis=1)
    row_peak = lax.pmax(local_peak, "ctx")
    expsum = jnp.sum(jnp.exp(logits - row_peak[:, None]), axis=1)
    expsum, picked = lax.psum((expsum, picked), "ctx")
    lse = row_peak + jnp.log(expsum)
    grad_logits = (jnp.exp(logits - lse[:, None]) - target_hit.astype(jnp.float32)).astype(
        jnp.bfloat16
    )
    loss_part = jnp.sum(lse - picked)
    loss = loss_part / total_rows
    grad_normed = lax.psum_scatter(
        lax.dot_general(
            grad_logits, head_weight, (((1,), (1,)), ((), ())), preferred_element_type=jnp.float32
        ),
        "ctx",
        scatter_dimension=0,
        tiled=True,
    ).astype(jnp.bfloat16)
    grad_head = lax.dot_general(
        block, grad_logits, (((0,), (0,)), ((), ())), preferred_element_type=jnp.float32
    ).astype(jnp.bfloat16)
    return (loss, grad_normed, grad_head)


def solution(mesh):
    placed = (
        P("ctx", "tp"),
        P("ctx", "tp"),
        P("ctx", "tp"),
        P(),
        P(),
        P("tp", None, "ctx", None),
        P(None, "tp", "ctx", None),
        P("tp", "ctx", None),
        P("tp", "ctx"),
    )
    return jax.shard_map(
        per_device,
        mesh=mesh,
        in_specs=placed,
        out_specs=(P(), P("ctx", "tp"), P("tp", "ctx")),
        check_vma=False,
    )
```

profile of v0, /device:TPU:0, one launch (start us, length us, event | category | flops | bytes accessed | tf_op | source)
XLA Modules:
  0.0 624.3 jit_solution(13391071444253082746)
XLA Ops:
  7.2 0.0 all-gather.5.cloned.1.call-start
  7.2 0.7 all-gather.5.cloned.1.call-update
  7.9 0.0 all-gather.7.cloned.1.call-start
  8.0 0.7 all-gather.7.cloned.1.call-update
  8.7 0.0 all-gather.9.cloned.1.call-start
  8.7 0.8 select_reduce_fusion.2
  9.5 0.1 dynamic_slice.3
  9.6 0.9 select_reduce_fusion.1
  10.5 0.8 broadcast_compare_fusion
  11.9 0.9 copy.28
  12.8 43.5 %all-gather.5.cloned.1.call-done = bf16[4096,256]{1,0:T(8,128)(2,1)} async-done(((bf16[128,256]{1,0:T(8,128)(2,1)}), bf16[4096,256]{1,0:T(8,128)(2,1)}) %all-gather.5.cloned.1.call-update) | async-done | bytes 2097168 | tf_op jit(solution)/shard_map/all_gather | solution.py:99
  56.2 5.8 conditional.2
  56.2 2.5 reshape.82
  58.8 1.0 fusion.48
  59.8 0.6 broadcast_maximum_fusion
  60.4 1.7 select_reduce_fusion
  62.1 39.3 %all-gather.7.cloned.1.call-done = bf16[4096,256]{1,0:T(8,128)(2,1)} async-done(((bf16[128,256]{1,0:T(8,128)(2,1)}), bf16[4096,256]{1,0:T(8,128)(2,1)}) %all-gather.7.cloned.1.call-update) | async-done | bytes 2097168 | tf_op jit(solution)/shard_map/all_gather | solution.py:100
  101.3 10.5 %conditional.3 = (bf16[16,2,8,128]{3,0,2,1:T(8,128)(2,1)S(1)}) conditional(s32[]{:T(128)} %convert_element_type.33, () %tuple.22, (pred[16,4096]{1,0:T(8,128)(4,1)S(1)}, bf16[4096,256]{1,0:T(8,128)(2,1)}, bf16[16,2,8,128]{3,2,1,0:T(8,128)(2,1)S(1)}, f32[2,8,16]{2,1,0:T(8,128)}, f32[2,8,16]{2,1,0:T(8,128)S(1)}, ...), branch_computations={%region_7.8_spmd, %region_8.9_spmd} | conditional | flops 543162368 | bytes 21170212 | solution.py:64
  101.3 4.1 reshape.95
  105.4 2.0 reshape.84
  107.4 4.4 fusion.12
  111.9 0.6 copy.50
  112.5 0.0 all-gather.9.cloned.1.call-update
  112.5 0.0 reduce-scatter.3.cloned.1.call-start
  112.6 42.9 %all-gather.9.cloned.1.call-done = bf16[512,2048]{1,0:T(8,128)(2,1)} async-done(((bf16[16,2048]{1,0:T(8,128)(2,1)}), bf16[512,2048]{1,0:T(8,128)(2,1)}) %all-gather.9.cloned.1.call-update) | async-done | bytes 2097168 | tf_op jit(solution)/shard_map/all_gather | solution.py:109
  155.5 3.1 fusion.25
  158.6 0.0 reduce-scatter.3.cloned.1.call-update
  158.6 0.0 all-gather.11.cloned.1.call-start
  158.7 21.3 %reduce-scatter.3.cloned.1.call-done = f32[512,1,64]{0,2,1:T(8,128)} async-done(((f32[512,4,64]{0,2,1:T(8,128)}), f32[512,1,64]{0,2,1:T(8,128)}) %reduce-scatter.3.cloned.1.call-update) | async-done | bytes 131088 | tf_op jit(solution)/shard_map/reduce_scatter | solution.py:113
  180.0 0.9 multiply_reduce_fusion
  180.9 65.0 %psum.28 = f32[512]{0:T(512)S(1)} all-reduce(f32[512]{0:T(512)S(1)} %multiply_reduce_fusion), channel_id=1, replica_groups=mesh['ctx'=32,'tp'=4] {'ctx','tp'}, use_global_device_ids=true, to_apply=%region_11.12 | all-reduce | flops 512 | bytes 4096 | tf_op jit(solution)/shard_map/psum | solution.py:119
  245.9 1.6 multiply_convert_fusion
  247.5 0.0 all-gather.11.cloned.1.call-update
  247.6 0.0 all-reduce.3.cloned.1.call-start
  247.6 39.5 %all-gather.11.cloned.1.call-done = bf16[512,2048]{0,1:T(8,128)(2,1)} async-done(((bf16[512,64]{0,1:T(8,128)(2,1)}), bf16[512,2048]{0,1:T(8,128)(2,1)}) %all-gather.11.cloned.1.call-update) | async-done | bytes 2097168 | tf_op jit(solution)/shard_map/all_gather | solution.py:123
  287.1 10.6 %fusion.49 = f32[512,2048]{1,0:T(8,128)} fusion(bf16[512,2048]{0,1:T(8,128)(2,1)} %all-gather.11.cloned.1.call-done, bf16[2048,2048]{1,0:T(8,128)(2,1)} %param.21), kind=kOutput, calls=%fused_computation.72 | convolution fusion | flops 4294967296 | bytes 14680064 | tf_op jit(solution)/shard_map/dot_general | solution.py:126
  297.7 0.0 reduce-scatter.5.cloned.1.call-start
  297.8 92.5 %all-reduce.3.cloned.1.call-done = f32[512,2048]{1,0:T(8,128)} async-done(((f32[512,2048]{1,0:T(8,128)}), f32[512,2048]{1,0:T(8,128)}) %all-reduce.3.cloned.1.call-update) | async-done | bytes 4194320 | tf_op jit(solution)/shard_map/psum | solution.py:126
  390.3 2.5 reduce_max.18
  392.7 67.0 %pmax.7 = f32[512]{0:T(512)S(1)} all-reduce(f32[512]{0:T(512)S(1)} %reduce_max.18), channel_id=1, replica_groups=mesh['ctx'=32,'tp'=4] {'ctx'}, use_global_device_ids=true, to_apply=%region_14.15 | all-reduce | flops 512 | bytes 4096 | tf_op jit(solution)/shard_map/pmax | solution.py:131
  459.7 3.4 fusion.22
  463.1 62.7 %all-reduce = (f32[512]{0:T(512)S(1)}, f32[512]{0:T(512)S(1)}) all-reduce(f32[512]{0:T(512)S(1)} %get-tuple-element.44, f32[512]{0:T(512)S(1)} %get-tuple-element.43), channel_id=1, replica_groups=mesh['ctx'=32,'tp'=4] {'ctx'}, use_global_device_ids=true, to_apply=%region_16.17 | all-reduce | flops 1024 | bytes 8192 | tf_op jit(solution)/shard_map/psum | solution.py:133
  525.8 0.6 subtract_reduce_fusion
  526.4 11.2 %fusion.46 = f32[512,2048]{1,0:T(8,128)} fusion(bf16[2048,2048]{1,0:T(8,128)(2,1)} %param.21, f32[512,2048]{1,0:T(8,128)} %all-reduce.3.cloned.1.call-done, f32[512]{0:T(512)S(1)} %get-tuple-element.48, s32[2048]{0:T(1024)S(1)} %iota_add_fusion, s32[512]{0:T(512)S(1)} %copy-done.3), kind=kOutput, calls=%fused_computation.70 | convolution fusion | flops 4300210176 | bytes 16789504 | tf_op jit(solution)/shard_map/dot_general | solution.py:141
  538.4 0.8 copy-done.5
  539.2 9.3 %convolution_convert_fusion = bf16[2048,2048]{1,0:T(8,128)(2,1)} fusion(bf16[512,2048]{0,1:T(8,128)(2,1)S(1)} %copy-done.5, f32[512,2048]{1,0:T(8,128)} %all-reduce.3.cloned.1.call-done, f32[512]{0:T(512)S(1)} %get-tuple-element.48, s32[2048]{0:T(1024)S(1)} %iota_add_fusion, s32[512]{0:T(512)S(1)} %copy-done.3), kind=kOutput, calls=%fused_computation.22 | convolution fusion | flops 4304404480 | bytes 14692352 | tf_op jit(solution)/shard_map/dot_general | solution.py:148
  548.5 66.3 %reduce-scatter.5.cloned.1.call-done = f32[16,2048]{1,0:T(8,128)} async-done(((f32[512,2048]{1,0:T(8,128)}), f32[16,2048]{1,0:T(8,128)}) %reduce-scatter.5.cloned.1.call-update) | async-done | bytes 131088 | tf_op jit(solution)/shard_map/reduce_scatter | solution.py:140
  614.8 1.5 convert_element_type.38
  (20 shorter events, 0.1 us)
Async XLA Ops:
  7.2 148.3 %copy-start = (bf16[2048,4,1,64]{0,3,2,1:T(8,128)(2,1)S(1)}, bf16[2048,4,1,64]{0,3,2,1:T(8,128)(2,1)}, u32[]{:S(2)}) copy-start(bf16[2048,4,1,64]{0,3,2,1:T(8,128)(2,1)} %param.18) | copy-start | bytes 3145732
  7.2 49.0 %all-gather.5.cloned.1.call-start = ((), (), s32[]{:S(2)}) async-start(), calls=%async_computation.2 | async-start | bytes 2162688 | tf_op jit(solution)/shard_map/all_gather | solution.py:99
  7.9 93.4 %all-gather.7.cloned.1.call-start = ((), (), s32[]{:S(2)}) async-start(), calls=%async_computation.3 | async-start | bytes 2162688 | tf_op jit(solution)/shard_map/all_gather | solution.py:100
  8.7 146.8 %all-gather.9.cloned.1.call-start = ((), (), s32[]{:S(2)}) async-start(), calls=%async_computation.4 | async-start | bytes 2162688 | tf_op jit(solution)/shard_map/all_gather | solution.py:109
  101.3 4.1 copy-start.1
  111.8 68.2 %copy-start.2 = (bf16[512,1,1,64]{0,3,2,1:T(8,128)(2,1)S(1)}, bf16[512,1,1,64]{0,3,2,1:T(8,128)(2,1)}, u32[]{:S(2)}) copy-start(bf16[512,1,1,64]{0,3,2,1:T(8,128)(2,1)} %param.19) | copy-start | bytes 196612
  111.8 134.1 %copy-start.4 = (f32[1,1,64]{2,1,0:T(1,128)S(1)}, f32[1,1,64]{2,1,0:T(1,128)}, u32[]{:S(2)}) copy-start(f32[1,1,64]{2,1,0:T(1,128)} %param.20) | copy-start | bytes 772
  112.5 67.4 %reduce-scatter.3.cloned.1.call-start = ((), (), s32[]{:S(2)}) async-start(), calls=%async_computation.5 | async-start | bytes 655360 | tf_op jit(solution)/shard_map/reduce_scatter | solution.py:113
  158.6 128.4 %all-gather.11.cloned.1.call-start = ((), (), s32[]{:S(2)}) async-start(), calls=%async_computation.6 | async-start | bytes 2162688 | tf_op jit(solution)/shard_map/all_gather | solution.py:123
  247.6 142.7 %all-reduce.3.cloned.1.call-start = ((), (), s32[]{:S(2)}) async-start(), calls=%async_computation.7 | async-start | bytes 8388608 | tf_op jit(solution)/shard_map/psum | solution.py:126
  297.7 162.0 %copy-start.3 = (s32[512]{0:T(512)S(1)}, s32[512]{0:T(512)}, u32[]{:S(2)}) copy-start(s32[512]{0:T(512)} %param.17) | copy-start | bytes 6148
  297.7 317.1 %reduce-scatter.5.cloned.1.call-start = ((), (), s32[]{:S(2)}) async-start(), calls=%async_computation.8 | async-start | bytes 4325376 | tf_op jit(solution)/shard_map/reduce_scatter | solution.py:140
  537.6 1.6 copy-start.5
Sparse Core Ops, SparseCore 0:
  10.3 45.9 all-gather.4
  58.5 42.7 all-gather.6
  112.7 42.7 all-gather.8
  158.8 21.1 reduce-scatter.2
  247.7 39.3 all-gather.10
  297.8 92.4 all-reduce.2
  537.7 77.0 reduce-scatter.4
where the time goes:
time: 625 us; the launch traced here: 624 us
  waiting for transfers between devices  347 us (56%)
  blocking collectives  195 us (31%)
  matrix products  39.6 us (6%)
  between operations  16.8 us (3%)
  other arithmetic  15.3 us (2%)
  local copies, waits for them, and re-layouts  11.1 us (2%)
    psum x1, waiting for transfers between devices, per_device(): lax.psum(jnp.dot(block, head_weight, preferred_element_type=jnp.float32),...  92.5 us
    pmax x1, blocking collectives, per_device(): row_peak = lax.pmax(local_peak, 'ctx')  67 us
    reduce_scatter x1, waiting for transfers between devices, per_device(): lax.psum_scatter(lax.dot_general(grad_logits, head_weight, (((1,), (1,)),...  66.3 us
    psum x1, blocking collectives, per_device(): squares = lax.psum(jnp.sum(hidden * hidden, axis=1), ('ctx', 'tp'))  65 us
    psum x1, blocking collectives, per_device(): expsum, picked = lax.psum((expsum, picked), 'ctx')  62.7 us
    all_gather x1, waiting for transfers between devices, per_device(): lax.all_gather(rotated_keys, 'ctx', axis=0, tiled=True)  43.5 us
    all_gather x1, waiting for transfers between devices, per_device(): lax.all_gather(attn, 'ctx', axis=0, tiled=True)  42.9 us
    all_gather x1, waiting for transfers between devices, per_device(): block = lax.all_gather(normed, 'ctx', axis=1, tiled=True)  39.5 us
  transfers between devices with their start and end apart: 7, of which 7 were waited for; matrix products, arithmetic and copies ran while one was open for 3% of the time, Pallas kernels for 0%

commit v1 on v0

v1 whole, which is shorter than its diff:
```python
import jax
import jax.numpy as jnp
from jax import lax
from jax.sharding import Mesh
from jax.sharding import PartitionSpec as P

D = 8192
KEY_VALUE_HEADS = 8
HEAD_SIZE = 128

EPSILON = 1e-05
MASKED = -1e30

NX, NY, NC, NZ = 4, 4, 2, 4
CTX = ("x", "y", "c")
PLANE = ("x", "y")
CHIPS = ("x", "y", "z")
F32 = jnp.float32
BF16 = jnp.bfloat16
F16 = jnp.float16


def swap(value):
    return lax.ppermute(value, "c", [(0, 1), (1, 0)])


def exchange(value, axes):
    return lax.all_to_all(value, axes, 0, 0, tiled=True)


def spread(value, axes, count):
    copies = jnp.broadcast_to(value[None], (count,) + value.shape)
    return lax.all_to_all(copies, axes, 0, 0, tiled=True)


def pick(pair, index):
    return lax.dynamic_index_in_dim(pair, index, 0, keepdims=False)


def span_starts(span_order, repeat, span_rows):
    return jnp.repeat(span_order * span_rows, repeat, total_repeat_length=span_order.shape[0] * repeat)


def attend(grouped, keys, values, visible):
    scores = lax.dot_general(
        grouped, keys, (((1,), (1,)), ((), ())), preferred_element_type=F32
    ) * HEAD_SIZE ** (-0.5)
    scores = jnp.where(visible, scores, MASKED)
    peak = jnp.max(scores, axis=-1, keepdims=True)
    expo = jnp.exp(scores - peak)
    weights = (expo / jnp.sum(expo, axis=-1, keepdims=True)).astype(BF16)
    return jnp.dot(weights, values, preferred_element_type=F32).astype(BF16)


def per_device(
    queries,
    rotated_keys,
    value_rows,
    span_order,
    targets,
    out_weight,
    residual,
    norm_gain,
    head_weight,
):
    x, y, c, z = (lax.axis_index(a) for a in ("x", "y", "c", "z"))
    xy = x * NY + y
    first = c == 0
    q_dev = queries.shape[0]
    tok_dev = rotated_keys.shape[0]
    planes = NX * NY
    span_rows = tok_dev // 2
    q_span = q_dev // 2
    total_rows = q_dev * planes * NC
    total_keys = tok_dev * planes * NC
    half_rows = total_rows // NC

    key_pair = rotated_keys.reshape(tok_dev, NC, HEAD_SIZE).transpose(1, 0, 2)
    value_pair = value_rows.reshape(tok_dev, NC, HEAD_SIZE).transpose(1, 0, 2)
    packed = jnp.concatenate([key_pair, value_pair], axis=2)
    packed = jnp.broadcast_to(packed[None], (planes,) + packed.shape)
    gathered = exchange(packed.reshape(planes * NC, tok_dev, 2 * HEAD_SIZE), CTX)
    gathered = gathered.reshape(total_keys, 2 * HEAD_SIZE)
    keys, values = gathered[:, :HEAD_SIZE], gathered[:, HEAD_SIZE:]

    head_width = queries.shape[1] // NC
    query_pair = queries.reshape(q_dev, NC, head_width).transpose(1, 0, 2)
    q_own = pick(query_pair, c)
    q_got = swap(pick(query_pair, 1 - c))
    chip_queries = jnp.where(
        first, jnp.concatenate([q_own, q_got]), jnp.concatenate([q_got, q_own])
    )
    chip_rows = 2 * q_dev
    group = head_width // HEAD_SIZE
    grouped = (
        chip_queries.reshape(chip_rows, group, HEAD_SIZE)
        .transpose(1, 0, 2)
        .reshape(group * chip_rows, HEAD_SIZE)
    )

    slice_width = out_weight.shape[3]
    out_pair = out_weight.reshape(NC, out_weight.shape[0] // NC, NZ, slice_width)
    out_own = pick(out_pair, c)
    out_got = swap(pick(out_pair, 1 - c))
    out_low = jnp.where(first, out_own, out_got)
    out_high = jnp.where(first, out_got, out_own)
    out_both = jnp.stack([out_low, out_high], axis=2).reshape(-1, NZ * NC * slice_width)
    gain_own = norm_gain.reshape(slice_width)
    gain_got = swap(gain_own)
    gain = jnp.concatenate(
        [jnp.where(first, gain_own, gain_got), jnp.where(first, gain_got, gain_own)]
    )
    head_got = swap(head_weight)

    key_pos = span_starts(span_order, span_rows, span_rows) + jnp.arange(total_keys) % span_rows
    query_pos = (
        span_starts(span_order, q_span, span_rows)
        + (span_rows - q_span)
        + jnp.arange(total_rows) % q_span
    )
    chip_pos = lax.dynamic_slice_in_dim(query_pos, xy * chip_rows, chip_rows)
    row_pos = jnp.broadcast_to(chip_pos[None], (group, chip_rows)).reshape(-1)
    visible = key_pos[None, :] <= row_pos[:, None]
    attn = attend(grouped, keys, values, visible)
    attn = attn.reshape(group, chip_rows, HEAD_SIZE).transpose(1, 0, 2).reshape(chip_rows, -1)
    attn_all = spread(attn, PLANE, planes).reshape(total_rows, -1)

    mixed = jnp.dot(attn_all, out_both, preferred_element_type=F32)
    mine = (jnp.arange(NZ)[:, None] == z) & (jnp.arange(NC)[None, :] == c)
    own_part = jnp.where(
        mine[None, :, :, None],
        residual.reshape(total_rows, 1, 1, slice_width).astype(F32),
        0.0,
    ).reshape(total_rows, -1)
    mixed = mixed + own_part
    mixed_pair = mixed.reshape(planes, NC, q_dev, -1).transpose(1, 0, 2, 3)
    mixed = pick(mixed_pair, c) + swap(pick(mixed_pair, 1 - c))
    width = NC * slice_width
    mixed = mixed.reshape(half_rows, NZ, width).transpose(1, 0, 2)
    hidden = jnp.sum(exchange(mixed, "z"), axis=0)

    square_part = jnp.sum(hidden * hidden, axis=1).reshape(-1, 128)
    squares = jnp.sum(spread(square_part, CHIPS, planes * NZ).reshape(planes * NZ, half_rows), axis=0)
    normed = (hidden * lax.rsqrt(squares / D + EPSILON)[:, None] * gain[None, :]).astype(BF16)
    block = (
        spread(normed, PLANE, planes)
        .reshape(planes, half_rows, width)
        .transpose(1, 0, 2)
        .reshape(half_rows, -1)
    )
    block_got = swap(block)

    vocab_width = head_weight.shape[1]
    z_rows = half_rows // NZ

    def summed_logits(weight):
        part = jnp.dot(block, weight, preferred_element_type=F32).astype(F16)
        parts = exchange(part, "z").reshape(NZ, z_rows, vocab_width)
        return jnp.sum(parts.astype(F32), axis=0)

    logits = (summed_logits(head_weight), summed_logits(head_got))
    row_targets = pick(targets.reshape(planes, NC, q_dev).transpose(1, 0, 2), c).reshape(-1)
    row_targets = lax.dynamic_slice_in_dim(row_targets, z * z_rows, z_rows)
    columns = jnp.arange(vocab_width, dtype=jnp.int32)[None, :]
    hits = tuple(
        columns + (xy * NC + core) * vocab_width == row_targets[:, None] for core in (c, 1 - c)
    )
    peak = jnp.maximum(jnp.max(logits[0], axis=1), jnp.max(logits[1], axis=1))
    total = sum(jnp.sum(jnp.exp(part - peak[:, None]), axis=1) for part in logits)
    picked = sum(
        jnp.sum(jnp.where(hit, part, 0.0), axis=1) for hit, part in zip(hits, logits)
    )
    stats = jnp.pad(jnp.stack([peak, total, picked]), ((0, 5), (0, 128 - z_rows)))
    stats = spread(stats, CHIPS, planes * NZ).reshape(planes, NZ, 8, 128)[:, :, :3, :z_rows]
    row_peak = jnp.max(stats[:, :, 0], axis=0)
    row_total = jnp.sum(stats[:, :, 1] * jnp.exp(stats[:, :, 0] - row_peak[None]), axis=0)
    row_lse = row_peak + jnp.log(row_total)
    row_loss = jnp.sum(row_lse - jnp.sum(stats[:, :, 2], axis=0)).reshape(1, 1)
    loss = ((row_loss + swap(row_loss)) / total_rows).reshape(())
    lse = pick(row_lse, z)

    grads = [
        (jnp.exp(part - lse[:, None]) - hit.astype(F32)).astype(BF16)
        for hit, part in zip(hits, logits)
    ]
    grad_own, grad_far = (
        spread(g, "z", NZ).reshape(half_rows, vocab_width) for g in grads
    )
    grad_got = swap(grad_far)
    transposed = (((1,), (1,)), ((), ()))
    grad_rows = lax.dot_general(
        grad_own, head_weight, transposed, preferred_element_type=F32
    ) + lax.dot_general(grad_far, head_got, transposed, preferred_element_type=F32)
    grad_parts = exchange(grad_rows.astype(BF16), PLANE).reshape(planes, q_dev, -1)
    grad_normed = jnp.sum(grad_parts.astype(F32), axis=0).astype(BF16)
    grad_head = lax.dot_general(
        jnp.concatenate([block, block_got]),
        jnp.concatenate([grad_own, grad_got]),
        (((0,), (0,)), ((), ())),
        preferred_element_type=F32,
    ).astype(BF16)
    return (loss, grad_normed, grad_head)


def solution(mesh):
    fine = Mesh(mesh.devices.reshape(NX, NY, NC, NZ), ("x", "y", "c", "z"))
    placed = (
        P(CTX, "z"),
        P(CTX, "z"),
        P(CTX, "z"),
        P(),
        P(),
        P("z", None, CTX, None),
        P(None, "z", CTX, None),
        P("z", CTX, None),
        P("z", CTX),
    )
    return jax.shard_map(
        per_device,
        mesh=fine,
        in_specs=placed,
        out_specs=(P(), P(CTX, "z"), P("z", CTX)),
        check_vma=False,
    )
```

time: 625 us -> 320 us (0.51)
  waiting for transfers between devices: 347 us -> 80.3 us
  blocking collectives: 195 us -> 31.6 us
  other arithmetic: 15.3 us -> 90.2 us
  starting transfers between devices: 0.28 us -> 48.7 us
  between operations: 16.8 us -> 3.64 us
  local copies, waits for them, and re-layouts: 11.1 us -> 19.8 us
    all_gather x4 -> x0, waiting for transfers between devices: 165 us -> none  [the longest x1 43.5 us: per_device(): lax.all_gather(rotated_keys, 'ctx', axis=0, tiled=True)]
    psum x2 -> x0, blocking collectives: 128 us -> none  [the longest x1 65 us: per_device(): squares = lax.psum(jnp.sum(hidden * hidden, axis=1), ('ctx', 'tp'))]
    psum x1 -> x0, waiting for transfers between devices: 92.5 us -> none  [per_device(): lax.psum(jnp.dot(block, head_weight, preferred_element_type=jnp.float32),...]
    reduce_scatter x2 -> x0, waiting for transfers between devices: 87.6 us -> none  [the longest x1 66.3 us: per_device(): lax.psum_scatter(lax.dot_general(grad_logits, head_weight, (((1,), (1,)),...]
    all_to_all x0 -> x9, waiting for transfers between devices: none -> 76.3 us  [the longest x5 38.9 us: exchange(): return lax.all_to_all(value, axes, 0, 0, tiled=True)]
    add x3 -> x6, other arithmetic: 0.02 us -> 71.3 us  [the longest x1 35.7 us: per_device(): span_starts(span_order, span_rows, span_rows)]
    pmax x1 -> x0, blocking collectives: 67 us -> none  [per_device(): row_peak = lax.pmax(local_peak, 'ctx')]
    all_to_all x0 -> x9, starting transfers between devices: none -> 47.1 us  [the longest x5 24.4 us: exchange(): return lax.all_to_all(value, axes, 0, 0, tiled=True)]
  transfers between devices with their start and end apart: 7 -> 17, of which waited for: 7 -> 11; matrix products, arithmetic and copies ran while one was open for 3% -> 43% of each run, Pallas kernels for 0% -> 0%
where the time goes in v1:
time: 320 us; the launch traced here: 317 us
  other arithmetic  90.2 us (28%)
  waiting for transfers between devices  80.3 us (25%)
  starting transfers between devices  48.7 us (15%)
  matrix products  42.7 us (13%)
  blocking collectives  31.6 us (10%)
  local copies, waits for them, and re-layouts  19.8 us (6%)
  between operations  3.64 us (1%)
    all_to_all x5, waiting for transfers between devices, exchange(): return lax.all_to_all(value, axes, 0, 0, tiled=True)  38.9 us
    all_to_all x4, waiting for transfers between devices, spread(): return lax.all_to_all(copies, axes, 0, 0, tiled=True)  37.4 us
    add x1, other arithmetic, per_device(): span_starts(span_order, span_rows, span_rows)  35.7 us
    add x1, other arithmetic, per_device(): span_starts(span_order, q_span, span_rows) + (span_rows - q_span)  35.5 us
    all_to_all x2, blocking collectives, spread(): return lax.all_to_all(copies, axes, 0, 0, tiled=True)  31.6 us
    all_to_all x5, starting transfers between devices, exchange(): return lax.all_to_all(value, axes, 0, 0, tiled=True)  24.4 us
    all_to_all x4, starting transfers between devices, spread(): return lax.all_to_all(copies, axes, 0, 0, tiled=True)  22.7 us
    dot_general x2, matrix products, summed_logits(): part = jnp.dot(block, weight, preferred_element_type=F32).astype(F16)  13.4 us
  transfers between devices with their start and end apart: 17, of which 11 were waited for; matrix products, arithmetic and copies ran while one was open for 43% of the time, Pallas kernels for 0%

profile of v1, /device:TPU:0, one launch (start us, length us, event | category | flops | bytes accessed | tf_op | source)
XLA Modules:
  0.0 316.9 jit_solution(14905105586313071181)
XLA Ops:
  0.6 1.0 reshape.516
  2.0 0.9 reshape.519
  2.9 0.9 reshape.518
  3.9 1.6 broadcast_in_dim.138
  5.5 7.7 %all-to-all-start = ((bf16[32,128,256]{2,1,0:T(8,128)(2,1)}), bf16[32,128,256]{2,1,0:T(8,128)(2,1)}, u32[]{:S(2)}, u32[]{:S(2)}) async-start(bf16[32,128,256]{2,1,0:T(8,128)(2,1)} %bitcast.78), calls=%async_computation | async-start | bytes 4194304 | tf_op jit(solution)/shard_map/all_to_all | solution.py:28
  14.0 2.2 constant_dynamic-slice_fusion.2
  16.1 1.0 copy.96
  19.2 4.2 %compare_select_fusion.11 = (s32[512,1]{0,1:T(1,128)S(1)}, s32[512,1]{0,1:T(1,128)S(1)}) fusion(s32[]{:T(128)} %bitcast.61, s32[]{:T(128)} %bitcast.62, s32[]{:T(128)} %bitcast.63, s32[]{:T(128)} %bitcast.64, s32[]{:T(128)} %bitcast.65, s32[]{:T(128)} %bitcast.67, s32[]{:T(128)} %bitcast.66, s32[512,1]{0,1:T(1,128)S(1)} %bitcast.208, s32[512,1]{0,1:T(1,128)S(1)} %bitcast.207), kind=kLoop, calls=%fused_computation.189 | loop fusion | flops 7168 | bytes 8220 | tf_op jit(solution)/shard_map/jit(_take)/gather | solution.py:41
  25.3 4.3 %compare_select_fusion.3 = (s32[4096,1]{0,1:T(1,128)S(1)}, s32[4096,1]{0,1:T(1,128)S(1)}) fusion(s32[]{:T(128)} %bitcast.61, s32[]{:T(128)} %bitcast.62, s32[]{:T(128)} %bitcast.63, s32[]{:T(128)} %bitcast.64, s32[]{:T(128)} %bitcast.65, s32[]{:T(128)} %bitcast.67, s32[]{:T(128)} %bitcast.66, s32[4096,1]{0,1:T(1,128)S(1)} %bitcast.202, ...), kind=kLoop, calls=%fused_computation.109 | loop fusion | flops 57344 | bytes 65564 | tf_op jit(solution)/shard_map/jit(_take)/gather | solution.py:41
  29.5 2.9 compare_reduce_fusion.56
  32.5 35.7 %fusion.22 = s32[4096]{0:T(1024)S(1)} fusion(pred[4096]{0:T(1024)(128)(4,1)S(1)} %get-tuple-element.87, pred[4096]{0:T(1024)(128)(4,1)S(1)} %get-tuple-element.86, pred[4096]{0:T(1024)(128)(4,1)S(1)} %get-tuple-element.85, pred[4096]{0:T(1024)(128)(4,1)S(1)} %get-tuple-element.84, pred[4096]{0:T(1024)(128)(4,1)S(1)} %get-tuple-element.83, ...), kind=kLoop, calls=%fused_computation.122 | loop fusion | flops 299008 | bytes 282980 | tf_op jit(solution)/shard_map/add | solution.py:115
  68.2 35.5 %fusion.26 = s32[512]{0:T(512)S(1)} fusion(pred[512]{0:T(512)(128)(4,1)S(1)} %get-tuple-element.144, pred[512]{0:T(512)(128)(4,1)S(1)} %get-tuple-element.143, pred[512]{0:T(512)(128)(4,1)S(1)} %get-tuple-element.142, pred[512]{0:T(512)(128)(4,1)S(1)} %get-tuple-element.141, pred[512]{0:T(512)(128)(4,1)S(1)} %get-tuple-element.140, ...), kind=kLoop, calls=%fused_computation.203 | loop fusion | flops 37888 | bytes 35572 | tf_op jit(solution)/shard_map/add | solution.py:117
  103.9 2.1 fusion.38
  106.8 2.3 fusion.10
  109.1 1.1 broadcast_in_dim.141
  110.2 7.0 %all-to-all-start.1 = ((bf16[16,32,1024]{2,1,0:T(8,128)(2,1)}), bf16[16,32,1024]{2,1,0:T(8,128)(2,1)S(1)}, u32[]{:S(2)}, u32[]{:S(2)}) async-start(bf16[16,32,1024]{2,1,0:T(8,128)(2,1)} %broadcast_in_dim.141), calls=%async_computation.1 | async-start | bytes 2097152 | tf_op jit(solution)/shard_map/all_to_all | solution.py:33
  117.3 1.2 broadcast_in_dim.147
  118.5 1.6 copy.70
  120.3 1.2 fusion.19
  121.7 13.6 %all-to-all-done.1 = bf16[16,32,1024]{2,1,0:T(8,128)(2,1)S(1)} async-done(((bf16[16,32,1024]{2,1,0:T(8,128)(2,1)}), bf16[16,32,1024]{2,1,0:T(8,128)(2,1)S(1)}, u32[]{:S(2)}, u32[]{:S(2)}) %all-to-all-start.1) | async-done | bytes 1048608 | tf_op jit(solution)/shard_map/all_to_all | solution.py:33
  136.2 1.9 collective-permute-done.2
  138.4 0.8 copy.71
  139.2 5.3 %all-to-all-start.2 = ((f32[4,256,128]{2,1,0:T(8,128)}), f32[4,256,128]{2,1,0:T(8,128)S(1)}, u32[]{:S(2)}, u32[]{:S(2)}) async-start(f32[4,256,128]{2,1,0:T(8,128)} %copy.71), calls=%async_computation.2 | async-start | bytes 1048576 | tf_op jit(solution)/shard_map/all_to_all | solution.py:28
  144.5 1.2 collective-permute-done.3
  145.7 8.6 %all-to-all-done.2 = f32[4,256,128]{2,1,0:T(8,128)S(1)} async-done(((f32[4,256,128]{2,1,0:T(8,128)}), f32[4,256,128]{2,1,0:T(8,128)S(1)}, u32[]{:S(2)}, u32[]{:S(2)}) %all-to-all-start.2) | async-done | bytes 524320 | tf_op jit(solution)/shard_map/all_to_all | solution.py:28
  155.1 5.0 %all-to-all-start.3 = ((f32[64,2,128]{2,1,0:T(2,128)}), f32[64,2,128]{2,1,0:T(2,128)S(1)}, u32[]{:S(2)}, u32[]{:S(2)}) async-start(f32[64,2,128]{2,1,0:T(2,128)} %broadcast_in_dim.151), calls=%async_computation.3 | async-start | bytes 131072 | tf_op jit(solution)/shard_map/all_to_all | solution.py:33
  160.2 9.5 %all-to-all-done.3 = f32[64,2,128]{2,1,0:T(2,128)S(1)} async-done(((f32[64,2,128]{2,1,0:T(2,128)}), f32[64,2,128]{2,1,0:T(2,128)S(1)}, u32[]{:S(2)}, u32[]{:S(2)}) %all-to-all-start.3) | async-done | bytes 65568 | tf_op jit(solution)/shard_map/all_to_all | solution.py:33
  170.1 18.3 %all_to_all.67 = bf16[16,256,128]{1,2,0:T(8,128)(2,1)S(1)} all-to-all(bf16[16,256,128]{1,2,0:T(8,128)(2,1)S(1)} %broadcast_in_dim.152), channel_id=1, replica_groups=mesh['x'=4,'y'=4,'c'=2,'z'=4] {'x','y'}, dimensions={0} | all-to-all | bytes 2097152 | tf_op jit(solution)/shard_map/all_to_all | solution.py:33
  188.5 6.7 %convolution_convert_fusion.2 = f16[256,2048]{1,0:T(8,128)(2,1)} fusion(bf16[256,2048]{0,1:T(8,128)(2,1)S(1)} %bitcast.175, bf16[2048,2048]{1,0:T(8,128)(2,1)} %param.21), kind=kOutput, calls=%fused_computation.9 | convolution fusion | flops 2148007936 | bytes 10485760 | tf_op jit(solution)/shard_map/dot_general | solution.py:157
  195.2 3.5 %all-to-all-start.5 = ((f16[4,64,2048]{2,1,0:T(8,128)(2,1)}), f16[4,64,2048]{2,1,0:T(8,128)(2,1)S(1)}, u32[]{:S(2)}, u32[]{:S(2)}) async-start(f16[4,64,2048]{2,1,0:T(8,128)(2,1)} %bitcast.97), calls=%async_computation.5 | async-start | bytes 2097152 | tf_op jit(solution)/shard_map/all_to_all | solution.py:28
  198.7 6.7 %convolution_convert_fusion.1 = f16[256,2048]{1,0:T(8,128)(2,1)} fusion(bf16[256,2048]{0,1:T(8,128)(2,1)S(1)} %bitcast.176, bf16[2048,2048]{1,0:T(8,128)(2,1)} %collective-permute-done.4), kind=kOutput, calls=%fused_computation.8 | convolution fusion | flops 2148007936 | bytes 10485760 | tf_op jit(solution)/shard_map/dot_general | solution.py:157
  205.4 4.3 %all-to-all-done.5 = f16[4,64,2048]{2,1,0:T(8,128)(2,1)S(1)} async-done(((f16[4,64,2048]{2,1,0:T(8,128)(2,1)}), f16[4,64,2048]{2,1,0:T(8,128)(2,1)S(1)}, u32[]{:S(2)}, u32[]{:S(2)}) %all-to-all-start.5) | async-done | bytes 1048608 | tf_op jit(solution)/shard_map/all_to_all | solution.py:28
  209.7 4.3 %all-to-all-start.6 = ((f16[4,64,2048]{2,1,0:T(8,128)(2,1)}), f16[4,64,2048]{2,1,0:T(8,128)(2,1)}, u32[]{:S(2)}, u32[]{:S(2)}) async-start(f16[4,64,2048]{2,1,0:T(8,128)(2,1)} %bitcast.99), calls=%async_computation.6 | async-start | bytes 2097152 | tf_op jit(solution)/shard_map/all_to_all | solution.py:28
  214.7 10.3 %all-to-all-done.6 = f16[4,64,2048]{2,1,0:T(8,128)(2,1)} async-done(((f16[4,64,2048]{2,1,0:T(8,128)(2,1)}), f16[4,64,2048]{2,1,0:T(8,128)(2,1)}, u32[]{:S(2)}, u32[]{:S(2)}) %all-to-all-start.6) | async-done | bytes 1048608 | tf_op jit(solution)/shard_map/all_to_all | solution.py:28
  224.9 1.5 convert_reduce_fusion
  227.7 6.4 %all-to-all-start.7 = ((f32[64,8,128]{2,1,0:T(8,128)}), f32[64,8,128]{2,1,0:T(8,128)S(1)}, u32[]{:S(2)}, u32[]{:S(2)}) async-start(f32[64,8,128]{2,1,0:T(8,128)} %broadcast_in_dim.154), calls=%async_computation.7 | async-start | bytes 524288 | tf_op jit(solution)/shard_map/all_to_all | solution.py:33
  234.1 10.4 %all-to-all-done.7 = f32[64,8,128]{2,1,0:T(8,128)S(1)} async-done(((f32[64,8,128]{2,1,0:T(8,128)}), f32[64,8,128]{2,1,0:T(8,128)S(1)}, u32[]{:S(2)}, u32[]{:S(2)}) %all-to-all-start.7) | async-done | bytes 262176 | tf_op jit(solution)/shard_map/all_to_all | solution.py:33
  245.8 13.3 %all_to_all.68 = bf16[4,64,2048]{2,1,0:T(8,128)(2,1)S(1)} all-to-all(bf16[4,64,2048]{2,1,0:T(8,128)(2,1)S(1)} %broadcast_in_dim.155), channel_id=1, replica_groups=mesh['x'=4,'y'=4,'c'=2,'z'=4] {'z'}, dimensions={0} | all-to-all | bytes 2097152 | tf_op jit(solution)/shard_map/all_to_all | solution.py:33
  259.1 1.1 broadcast_in_dim.156
  260.2 4.2 %all-to-all-start.9 = ((bf16[4,64,2048]{2,1,0:T(8,128)(2,1)}), bf16[4,64,2048]{2,1,0:T(8,128)(2,1)}, u32[]{:S(2)}, u32[]{:S(2)}) async-start(bf16[4,64,2048]{2,1,0:T(8,128)(2,1)} %broadcast_in_dim.156), calls=%async_computation.9 | async-start | bytes 2097152 | tf_op jit(solution)/shard_map/all_to_all | solution.py:33
  264.5 7.1 %fusion.39 = f32[256,2048]{1,0:T(8,128)} fusion(bf16[256,2048]{1,0:T(8,128)(2,1)S(1)} %bitcast.185, bf16[2048,2048]{1,0:T(8,128)(2,1)} %param.21), kind=kOutput, calls=%fused_computation.236 | convolution fusion | flops 2147483648 | bytes 11534336 | tf_op jit(solution)/shard_map/dot_general | solution.py:191
  271.6 3.8 %all-to-all-done.9 = bf16[4,64,2048]{2,1,0:T(8,128)(2,1)} async-done(((bf16[4,64,2048]{2,1,0:T(8,128)(2,1)}), bf16[4,64,2048]{2,1,0:T(8,128)(2,1)}, u32[]{:S(2)}, u32[]{:S(2)}) %all-to-all-start.9) | async-done | bytes 1048608 | tf_op jit(solution)/shard_map/all_to_all | solution.py:33
  275.4 7.6 %fusion.2 = bf16[256,2048]{1,0:T(8,128)(2,1)} fusion(f32[256,2048]{1,0:T(8,128)} %fusion.39, bf16[256,2048]{1,0:T(8,128)(2,1)} %bitcast.110, bf16[2048,2048]{1,0:T(8,128)(2,1)} %collective-permute-done.4), kind=kOutput, calls=%fused_computation.7 | convolution fusion | flops 2148532224 | bytes 12582912 | tf_op jit(solution)/shard_map/dot_general | solution.py:193
  283.0 3.7 %all-to-all-start.10 = ((bf16[16,16,2048]{2,1,0:T(8,128)(2,1)}), bf16[16,16,2048]{2,1,0:T(8,128)(2,1)S(1)}, u32[]{:S(2)}, u32[]{:S(2)}) async-start(bf16[16,16,2048]{2,1,0:T(8,128)(2,1)} %bitcast.187), calls=%async_computation.10 | async-start | bytes 2097152 | tf_op jit(solution)/shard_map/all_to_all | solution.py:28
  286.7 0.8 collective-permute-start.5
  287.5 1.0 collective-permute-done.5
  289.8 15.7 %all-to-all-done.10 = bf16[16,16,2048]{2,1,0:T(8,128)(2,1)S(1)} async-done(((bf16[16,16,2048]{2,1,0:T(8,128)(2,1)}), bf16[16,16,2048]{2,1,0:T(8,128)(2,1)S(1)}, u32[]{:S(2)}, u32[]{:S(2)}) %all-to-all-start.10) | async-done | bytes 1048608 | tf_op jit(solution)/shard_map/all_to_all | solution.py:28
  306.3 9.5 %convolution_convert_fusion = bf16[2048,2048]{1,0:T(8,128)(2,1)} fusion(bf16[256,2048]{0,1:T(8,128)(2,1)} %collective-permute-done.6, bf16[256,2048]{0,1:T(8,128)(2,1)S(1)} %bitcast.178, bf16[256,2048]{1,0:T(8,128)(2,1)} %collective-permute-done.7, bf16[256,2048]{1,0:T(8,128)(2,1)S(1)} %bitcast.186), kind=kOutput, calls=%fused_computation | convolution fusion | flops 4307550208 | bytes 12582912 | tf_op jit(solution)/shard_map/dot_general | solution.py:196
  (96 shorter events, 13.0 us)
Async XLA Ops:
  0.6 12.5 %copy-start = (bf16[2048,4,1,64]{0,3,2,1:T(8,128)(2,1)S(1)}, bf16[2048,4,1,64]{0,3,2,1:T(8,128)(2,1)}, u32[]{:S(2)}) copy-start(bf16[2048,4,1,64]{0,3,2,1:T(8,128)(2,1)} %param.18) | copy-start | bytes 3145732
  1.9 102.0 %collective-permute-start = (bf16[16,1024]{1,0:T(8,128)(2,1)S(1)}, bf16[16,1024]{1,0:T(8,128)(2,1)S(1)}, u32[]{:S(2)}, u32[]{:S(2)}) collective-permute-start(bf16[16,1024]{1,0:T(8,128)(2,1)S(1)} %bitcast.204), channel_id=1, source_target_pairs={{0,4},{4,0},{1,5},{5,1},{2,6},{6,2},{3,7},{7,3},{8,12},{12,8},{9,1... | collective-permute-start | bytes 98312 | tf_op jit(solution)/shard_map/ppermute | solution.py:24
  5.5 98.5 %all-to-all-start = ((bf16[32,128,256]{2,1,0:T(8,128)(2,1)}), bf16[32,128,256]{2,1,0:T(8,128)(2,1)}, u32[]{:S(2)}, u32[]{:S(2)}) async-start(bf16[32,128,256]{2,1,0:T(8,128)(2,1)} %bitcast.78), calls=%async_computation | async-start | bytes 4194304 | tf_op jit(solution)/shard_map/all_to_all | solution.py:28
  13.1 4.5 %copy-start.6 = (s32[64]{0:T(128)S(1)}, s32[64]{0:T(128)}, u32[]{:S(2)}) copy-start(s32[64]{0:T(128)} %param.16) | copy-start | bytes 772
  13.1 5.9 %copy-start.3 = (s32[4,128]{1,0:T(4,128)S(1)}, s32[4,128]{1,0:T(4,128)}, u32[]{:S(2)}) copy-start(s32[4,128]{1,0:T(4,128)} %constant.246.clone.1) | copy-start | bytes 6148
  13.1 5.9 %copy-start.2 = (s32[32,128]{1,0:T(8,128)S(1)}, s32[32,128]{1,0:T(8,128)}, u32[]{:S(2)}) copy-start(s32[32,128]{1,0:T(8,128)} %constant.239.clone.1) | copy-start | bytes 49156
  17.1 103.2 %collective-permute-start.1 = (bf16[1024,4,64]{0,2,1:T(8,128)(2,1)}, bf16[1024,4,64]{0,2,1:T(8,128)(2,1)}, u32[]{:S(2)}, u32[]{:S(2)}) collective-permute-start(bf16[1024,4,64]{0,2,1:T(8,128)(2,1)} %bitcast.172), channel_id=1, source_target_pairs={{0,4},{4,0},{1,5},{5,1},{2,6},{6,2},{3,7},{7,3},{8,12},{12,8},{9,1... | collective-permute-start | bytes 1572872 | tf_op jit(solution)/shard_map/ppermute | solution.py:24
  17.3 181.4 %collective-permute-start.4 = (bf16[2048,2048]{1,0:T(8,128)(2,1)}, bf16[2048,2048]{1,0:T(8,128)(2,1)}, u32[]{:S(2)}, u32[]{:S(2)}) collective-permute-start(bf16[2048,2048]{1,0:T(8,128)(2,1)} %param.21), channel_id=1, source_target_pairs={{0,4},{4,0},{1,5},{5,1},{2,6},{6,2},{3,7},{7,3},{8,12},{12,8},{9,1... | collective-permute-start | bytes 25165832 | tf_op jit(solution)/shard_map/ppermute | solution.py:24
  106.8 10.5 %copy-start.1 = (bf16[512,1,1,64]{0,3,2,1:T(8,128)(2,1)S(1)}, bf16[512,1,1,64]{0,3,2,1:T(8,128)(2,1)}, u32[]{:S(2)}) copy-start(bf16[512,1,1,64]{0,3,2,1:T(8,128)(2,1)} %param.19) | copy-start | bytes 196612
  110.2 25.1 %all-to-all-start.1 = ((bf16[16,32,1024]{2,1,0:T(8,128)(2,1)}), bf16[16,32,1024]{2,1,0:T(8,128)(2,1)S(1)}, u32[]{:S(2)}, u32[]{:S(2)}) async-start(bf16[16,32,1024]{2,1,0:T(8,128)(2,1)} %broadcast_in_dim.141), calls=%async_computation.1 | async-start | bytes 2097152 | tf_op jit(solution)/shard_map/all_to_all | solution.py:33
  135.3 9.2 %copy-start.5 = (f32[1,1,64]{2,1,0:T(1,128)S(1)}, f32[1,1,64]{2,1,0:T(1,128)}, u32[]{:S(2)}) copy-start(f32[1,1,64]{2,1,0:T(1,128)} %param.20) | copy-start | bytes 772
  136.1 2.0 collective-permute-start.2
  139.2 15.1 %all-to-all-start.2 = ((f32[4,256,128]{2,1,0:T(8,128)}), f32[4,256,128]{2,1,0:T(8,128)S(1)}, u32[]{:S(2)}, u32[]{:S(2)}) async-start(f32[4,256,128]{2,1,0:T(8,128)} %copy.71), calls=%async_computation.2 | async-start | bytes 1048576 | tf_op jit(solution)/shard_map/all_to_all | solution.py:28
  144.5 1.2 collective-permute-start.3
  155.1 14.6 %all-to-all-start.3 = ((f32[64,2,128]{2,1,0:T(2,128)}), f32[64,2,128]{2,1,0:T(2,128)S(1)}, u32[]{:S(2)}, u32[]{:S(2)}) async-start(f32[64,2,128]{2,1,0:T(2,128)} %broadcast_in_dim.151), calls=%async_computation.3 | async-start | bytes 131072 | tf_op jit(solution)/shard_map/all_to_all | solution.py:33
  195.2 14.6 %all-to-all-start.5 = ((f16[4,64,2048]{2,1,0:T(8,128)(2,1)}), f16[4,64,2048]{2,1,0:T(8,128)(2,1)S(1)}, u32[]{:S(2)}, u32[]{:S(2)}) async-start(f16[4,64,2048]{2,1,0:T(8,128)(2,1)} %bitcast.97), calls=%async_computation.5 | async-start | bytes 2097152 | tf_op jit(solution)/shard_map/all_to_all | solution.py:28
  198.7 15.3 %copy-start.4 = (s32[512]{0:T(512)S(1)}, s32[512]{0:T(512)}, u32[]{:S(2)}) copy-start(s32[512]{0:T(512)} %param.17) | copy-start | bytes 6148
  209.7 15.2 %all-to-all-start.6 = ((f16[4,64,2048]{2,1,0:T(8,128)(2,1)}), f16[4,64,2048]{2,1,0:T(8,128)(2,1)}, u32[]{:S(2)}, u32[]{:S(2)}) async-start(f16[4,64,2048]{2,1,0:T(8,128)(2,1)} %bitcast.99), calls=%async_computation.6 | async-start | bytes 2097152 | tf_op jit(solution)/shard_map/all_to_all | solution.py:28
  227.7 16.8 %all-to-all-start.7 = ((f32[64,8,128]{2,1,0:T(8,128)}), f32[64,8,128]{2,1,0:T(8,128)S(1)}, u32[]{:S(2)}, u32[]{:S(2)}) async-start(f32[64,8,128]{2,1,0:T(8,128)} %broadcast_in_dim.154), calls=%async_computation.7 | async-start | bytes 524288 | tf_op jit(solution)/shard_map/all_to_all | solution.py:33
  260.2 15.2 %all-to-all-start.9 = ((bf16[4,64,2048]{2,1,0:T(8,128)(2,1)}), bf16[4,64,2048]{2,1,0:T(8,128)(2,1)}, u32[]{:S(2)}, u32[]{:S(2)}) async-start(bf16[4,64,2048]{2,1,0:T(8,128)(2,1)} %broadcast_in_dim.156), calls=%async_computation.9 | async-start | bytes 2097152 | tf_op jit(solution)/shard_map/all_to_all | solution.py:33
  264.4 41.9 %collective-permute-start.6 = (bf16[256,2048]{0,1:T(8,128)(2,1)S(1)}, bf16[256,2048]{0,1:T(8,128)(2,1)}, u32[]{:S(2)}, u32[]{:S(2)}) collective-permute-start(bf16[256,2048]{0,1:T(8,128)(2,1)S(1)} %bitcast.177), channel_id=1, source_target_pairs={{0,4},{4,0},{1,5},{5,1},{2,6},{6,2},{3,7},{7,3},{8,12},{12,8},{9,1... | collective-permute-start | bytes 3145736 | tf_op jit(solution)/shard_map/ppermute | solution.py:24
  275.4 30.9 %collective-permute-start.7 = (bf16[256,2048]{1,0:T(8,128)(2,1)}, bf16[256,2048]{1,0:T(8,128)(2,1)}, u32[]{:S(2)}, u32[]{:S(2)}) collective-permute-start(bf16[256,2048]{1,0:T(8,128)(2,1)} %bitcast.110), channel_id=1, source_target_pairs={{0,4},{4,0},{1,5},{5,1},{2,6},{6,2},{3,7},{7,3},{8,12},{12,8},{9,1... | collective-permute-start | bytes 3145736 | tf_op jit(solution)/shard_map/ppermute | solution.py:24
  283.0 22.5 %all-to-all-start.10 = ((bf16[16,16,2048]{2,1,0:T(8,128)(2,1)}), bf16[16,16,2048]{2,1,0:T(8,128)(2,1)S(1)}, u32[]{:S(2)}, u32[]{:S(2)}) async-start(bf16[16,16,2048]{2,1,0:T(8,128)(2,1)} %bitcast.187), calls=%async_computation.10 | async-start | bytes 2097152 | tf_op jit(solution)/shard_map/all_to_all | solution.py:28
  286.7 1.8 collective-permute-start.5

commit v2 on v1

v2 whole, which is shorter than its diff:
```python
import jax
import jax.numpy as jnp
from jax import lax
from jax.experimental import pallas as pl
from jax.experimental.pallas import tpu as pltpu
from jax.sharding import Mesh
from jax.sharding import PartitionSpec as P

D = 8192
KEY_VALUE_HEADS = 8
HEAD_SIZE = 128

EPSILON = 1e-05
MASKED = -1e30

NX, NY, NC, NZ = 4, 4, 2, 4
CTX = ("x", "y", "c")
PLANE = ("x", "y")
CHIPS = ("x", "y", "z")
F32 = jnp.float32
BF16 = jnp.bfloat16
F16 = jnp.float16


def swap(value):
    return lax.ppermute(value, "c", [(0, 1), (1, 0)])


def exchange(value, axes):
    return lax.all_to_all(value, axes, 0, 0, tiled=True)


def spread(value, axes, count):
    copies = jnp.broadcast_to(value[None], (count,) + value.shape)
    return lax.all_to_all(copies, axes, 0, 0, tiled=True)


def pick(pair, index):
    return lax.dynamic_index_in_dim(pair, index, 0, keepdims=False)


def ring(value, step):
    return lax.ppermute(value, "z", [(i, (i + step) % NZ) for i in range(NZ)])


def rolled(parts, index):
    return [pick(parts, (index + k) % NZ) for k in range(NZ)]


def span_offsets(span_ref, base, count, index, rows):
    starts = jnp.full(index.shape, span_ref[base], jnp.int32)
    for k in range(1, count):
        starts = jnp.where(index >= k * rows, span_ref[base + k], starts)
    return starts


KEY_CHUNK = 512


def attention_body(span_ref, place_ref, query_ref, packed_ref, out_ref, score_ref):
    chip_rows, width = query_ref.shape
    group = width // HEAD_SIZE
    spans = span_ref.shape[0]
    total_keys = packed_ref.shape[0]
    span_rows = total_keys // spans
    chunk_spans = KEY_CHUNK // span_rows
    chip_spans = spans // (NX * NY)
    q_span = chip_rows // chip_spans
    chunks = total_keys // KEY_CHUNK
    rows = group * chip_rows
    query = jnp.concatenate(
        [query_ref[:, g * HEAD_SIZE : (g + 1) * HEAD_SIZE] for g in range(group)], axis=0
    )
    row = lax.broadcasted_iota(jnp.int32, (rows, 1), 0) % chip_rows
    starts = span_offsets(span_ref, place_ref[0] * chip_spans, chip_spans, row, q_span)
    query_pos = starts * span_rows + (span_rows - q_span) + row % q_span
    lane = lax.broadcasted_iota(jnp.int32, (1, KEY_CHUNK), 1)

    def score(i, peak):
        keys = packed_ref[pl.ds(i * KEY_CHUNK, KEY_CHUNK), :HEAD_SIZE]
        scores = lax.dot_general(
            query, keys, (((1,), (1,)), ((), ())), preferred_element_type=F32
        ) * HEAD_SIZE ** (-0.5)
        key_starts = span_offsets(span_ref, i * chunk_spans, chunk_spans, lane, span_rows)
        key_pos = key_starts * span_rows + lane % span_rows
        scores = jnp.where(key_pos <= query_pos, scores, MASKED)
        score_ref[i] = scores
        for k in range(KEY_CHUNK // 128):
            peak = jnp.maximum(peak, scores[:, k * 128 : (k + 1) * 128])
        return peak

    peak = lax.fori_loop(0, chunks, score, jnp.full((rows, 128), MASKED, F32))
    peak = jnp.max(peak, axis=1, keepdims=True)

    def expo(i, total):
        grown = jnp.exp(score_ref[i] - peak)
        score_ref[i] = grown
        for k in range(KEY_CHUNK // 128):
            total = total + grown[:, k * 128 : (k + 1) * 128]
        return total

    total = lax.fori_loop(0, chunks, expo, jnp.zeros((rows, 128), F32))
    inverse = 1.0 / jnp.sum(total, axis=1, keepdims=True)

    def weigh(i, acc):
        weights = (score_ref[i] * inverse).astype(BF16)
        values = packed_ref[pl.ds(i * KEY_CHUNK, KEY_CHUNK), HEAD_SIZE:]
        return acc + jnp.dot(weights, values, preferred_element_type=F32)

    acc = lax.fori_loop(0, chunks, weigh, jnp.zeros((rows, HEAD_SIZE), F32)).astype(BF16)
    for g in range(group):
        out_ref[:, g * HEAD_SIZE : (g + 1) * HEAD_SIZE] = acc[g * chip_rows : (g + 1) * chip_rows]


def attend(span_order, place, query, packed):
    rows = query.shape[0] * query.shape[1] // HEAD_SIZE
    chunks = packed.shape[0] // KEY_CHUNK
    return pl.pallas_call(
        attention_body,
        grid_spec=pltpu.PrefetchScalarGridSpec(
            num_scalar_prefetch=2,
            grid=(1,),
            in_specs=[
                pl.BlockSpec(query.shape, lambda i, s, p: (0, 0)),
                pl.BlockSpec(packed.shape, lambda i, s, p: (0, 0)),
            ],
            out_specs=pl.BlockSpec(query.shape, lambda i, s, p: (0, 0)),
            scratch_shapes=[pltpu.VMEM((chunks, rows, KEY_CHUNK), F32)],
        ),
        out_shape=jax.ShapeDtypeStruct(query.shape, BF16),
        name="attend",
    )(span_order, place, query, packed)


def per_device(
    queries,
    rotated_keys,
    value_rows,
    span_order,
    targets,
    out_weight,
    residual,
    norm_gain,
    head_weight,
):
    x, y, c, z = (lax.axis_index(a) for a in ("x", "y", "c", "z"))
    xy = x * NY + y
    first = c == 0
    q_dev = queries.shape[0]
    tok_dev = rotated_keys.shape[0]
    planes = NX * NY
    total_rows = q_dev * planes * NC
    total_keys = tok_dev * planes * NC
    half_rows = total_rows // NC

    packed = jnp.stack(
        [
            jnp.concatenate(
                [a[:, h * HEAD_SIZE : (h + 1) * HEAD_SIZE] for a in (rotated_keys, value_rows)], axis=1
            )
            for h in range(NC)
        ]
    )
    packed = jnp.broadcast_to(packed[None], (planes,) + packed.shape)
    packed = exchange(packed.reshape(planes * NC, tok_dev, 2 * HEAD_SIZE), CTX)
    packed = packed.reshape(total_keys, 2 * HEAD_SIZE)

    head_width = queries.shape[1] // NC
    q_low, q_high = queries[:, :head_width], queries[:, head_width:]
    q_own = jnp.where(first, q_low, q_high)
    q_got = swap(jnp.where(first, q_high, q_low))
    chip_queries = jnp.concatenate([jnp.where(first, q_own, q_got), jnp.where(first, q_got, q_own)])

    slice_width = out_weight.shape[3]
    out_pair = out_weight.reshape(NC, out_weight.shape[0] // NC, NZ, slice_width)
    out_own = pick(out_pair, c)
    out_got = swap(pick(out_pair, 1 - c))
    out_low = jnp.where(first, out_own, out_got)
    out_high = jnp.where(first, out_got, out_own)
    out_both = jnp.stack([out_low, out_high], axis=2).reshape(-1, NZ * NC * slice_width)
    gain_own = norm_gain.reshape(slice_width)
    gain_got = swap(gain_own)
    gain = jnp.concatenate(
        [jnp.where(first, gain_own, gain_got), jnp.where(first, gain_got, gain_own)]
    )
    head_got = swap(head_weight)

    attn = attend(span_order, xy.reshape(1), chip_queries, packed)
    attn_all = spread(attn, PLANE, planes).reshape(total_rows, -1)

    mixed = jnp.dot(attn_all, out_both, preferred_element_type=F32)
    mine = (jnp.arange(NZ)[:, None] == z) & (jnp.arange(NC)[None, :] == c)
    own_part = jnp.where(
        mine[None, :, :, None],
        residual.reshape(total_rows, 1, 1, slice_width).astype(F32),
        0.0,
    ).reshape(total_rows, -1)
    mixed = mixed + own_part
    mixed_pair = mixed.reshape(planes, NC, q_dev, -1).transpose(1, 0, 2, 3)
    mixed = pick(mixed_pair, c) + swap(pick(mixed_pair, 1 - c))
    width = NC * slice_width
    mixed = rolled(mixed.reshape(half_rows, NZ, width).transpose(1, 0, 2), z)
    hidden = mixed[0] + sum(ring(mixed[k], k) for k in range(1, NZ))

    square_part = jnp.sum(hidden * hidden, axis=1).reshape(-1, 128)
    squares = jnp.sum(spread(square_part, CHIPS, planes * NZ).reshape(planes * NZ, half_rows), axis=0)
    normed = (hidden * lax.rsqrt(squares / D + EPSILON)[:, None] * gain[None, :]).astype(BF16)
    z_rows = half_rows // NZ
    block = spread(normed, PLANE, planes).reshape(planes, NZ, z_rows, width)
    block = jnp.stack(rolled(block.transpose(1, 2, 0, 3), z)).reshape(half_rows, -1)
    block_got = swap(block)

    vocab_width = head_weight.shape[1]

    def summed_logits(weight):
        part = jnp.dot(block, weight, preferred_element_type=F32).astype(F16)
        part = part.reshape(NZ, z_rows, vocab_width)
        return part[0].astype(F32) + sum(ring(part[k], k).astype(F32) for k in range(1, NZ))

    logits = (summed_logits(head_weight), summed_logits(head_got))
    half_targets = pick(targets.reshape(planes, NC, q_dev).transpose(1, 0, 2), c)
    half_targets = jnp.concatenate(rolled(half_targets.reshape(NZ, z_rows), z))
    columns = jnp.arange(vocab_width, dtype=jnp.int32)[None, :]
    hits = tuple(
        columns + (xy * NC + core) * vocab_width == half_targets[:, None] for core in (c, 1 - c)
    )
    grown, stats = [], []
    for hit, part in zip(hits, logits):
        peak = jnp.max(part, axis=1)
        expo = jnp.exp(part - peak[:, None])
        grown.append(expo.astype(BF16))
        stats += [
            peak,
            jnp.sum(expo, axis=1),
            jnp.sum(jnp.where(hit[:z_rows], part, 0.0), axis=1),
        ]
    stats = jnp.pad(jnp.stack(stats), ((0, 2), (0, 128 - z_rows)))
    stats = spread(stats, CHIPS, planes * NZ).reshape(planes, NZ, 8, 128)[:, :, :6, :z_rows]
    stats = stats.reshape(planes, NZ, NC, 3, z_rows)
    row_peak = jnp.max(stats[:, :, :, 0], axis=(0, 2))
    row_total = jnp.sum(
        stats[:, :, :, 1] * jnp.exp(stats[:, :, :, 0] - row_peak[None, :, None]), axis=(0, 2)
    )
    row_lse = row_peak + jnp.log(row_total)
    row_loss = jnp.sum(row_lse - jnp.sum(stats[:, :, :, 2], axis=(0, 2))).reshape(1, 1)
    loss = ((row_loss + swap(row_loss)) / total_rows).reshape(())
    scales = jnp.exp(pick(stats, xy)[:, :, 0] - row_lse[:, None])

    def gathered_grads(part, hit, scale):
        whole = jnp.concatenate([part] + [ring(part, k) for k in range(NZ - 1, 0, -1)])
        scale = jnp.concatenate(rolled(scale, z))
        return (whole.astype(F32) * scale[:, None] - hit.astype(F32)).astype(BF16)

    grad_own, grad_far = (
        gathered_grads(grown[h], hits[h], scales[:, h]) for h in range(NC)
    )
    grad_got = swap(grad_far)
    transposed = (((1,), (1,)), ((), ()))
    grad_rows = lax.dot_general(
        grad_own, head_weight, transposed, preferred_element_type=F32
    ) + lax.dot_general(grad_far, head_got, transposed, preferred_element_type=F32)
    grad_rows = jnp.concatenate(rolled(grad_rows.astype(BF16).reshape(NZ, z_rows, -1), -z))
    grad_parts = exchange(grad_rows, PLANE).reshape(planes, q_dev, -1)
    grad_head = lax.dot_general(
        jnp.concatenate([block, block_got]),
        jnp.concatenate([grad_own, grad_got]),
        (((0,), (0,)), ((), ())),
        preferred_element_type=F32,
    ).astype(BF16)
    grad_parts, grad_head = lax.optimization_barrier((grad_parts, grad_head))
    grad_normed = jnp.sum(grad_parts.astype(F32), axis=0).astype(BF16)
    return (loss, grad_normed, grad_head)


def solution(mesh):
    fine = Mesh(mesh.devices.reshape(NX, NY, NC, NZ), ("x", "y", "c", "z"))
    placed = (
        P(CTX, "z"),
        P(CTX, "z"),
        P(CTX, "z"),
        P(),
        P(),
        P("z", None, CTX, None),
        P(None, "z", CTX, None),
        P("z", CTX, None),
        P("z", CTX),
    )
    return jax.shard_map(
        per_device,
        mesh=fine,
        in_specs=placed,
        out_specs=(P(), P(CTX, "z"), P("z", CTX)),
        check_vma=False,
    )
```

time: 320 us -> 241 us (0.75)
  other arithmetic: 90.2 us -> 10.8 us
  blocking collectives: 31.6 us -> 0 us
  waiting for transfers between devices: 80.3 us -> 106 us
  Pallas kernels: 0 us -> 7.62 us
  matrix products: 42.7 us -> 35.1 us
  starting transfers between devices: 48.7 us -> 55 us
    add x5 -> x1, other arithmetic: 71.2 us -> 0.01 us  [per_device(): columns + (xy * NC + core) * vocab_width == half_targets[:, None]]
    ppermute x0 -> x15, waiting for transfers between devices: none -> 33.2 us  [ring(): return lax.ppermute(value, 'z', [(i, (i + step) % NZ) for i in range(NZ)])]
    all_to_all x2 -> x0, blocking collectives: 31.6 us -> none  [spread(): return lax.all_to_all(copies, axes, 0, 0, tiled=True)]
    ppermute x0 -> x15, starting transfers between devices: none -> 20.9 us  [ring(): return lax.ppermute(value, 'z', [(i, (i + step) % NZ) for i in range(NZ)])]
    gather x4 -> x0, other arithmetic: 11.8 us -> none  [span_starts(): jnp.repeat(span_order * span_rows, repeat, total_repeat_length=span_order...]
    all_to_all x5 -> x2, starting transfers between devices: 24.4 us -> 13.7 us  [exchange(): return lax.all_to_all(value, axes, 0, 0, tiled=True)]
    all_to_all x5 -> x2, waiting for transfers between devices: 38.9 us -> 30.5 us  [exchange(): return lax.all_to_all(value, axes, 0, 0, tiled=True)]
    pallas_call x0 -> x1, Pallas kernels: none -> 7.62 us  [attend(): pl.pallas_call(attention_body, grid_spec=pltpu.PrefetchScalarGridSpec(num...]
  transfers between devices with their start and end apart: 17 -> 29, of which waited for: 11 -> 16; matrix products, arithmetic and copies ran while one was open for 43% -> 27% of each run, Pallas kernels for 0% -> 3%
where the time goes in v2:
time: 241 us; the launch traced here: 240 us
  waiting for transfers between devices  106 us (44%)
  starting transfers between devices  55 us (23%)
  matrix products  35.1 us (15%)
  local copies, waits for them, and re-layouts  21.6 us (9%)
  other arithmetic  10.8 us (4%)
  Pallas kernels  7.62 us (3%)
  between operations  3.7 us (2%)
    all_to_all x4, waiting for transfers between devices, spread(): return lax.all_to_all(copies, axes, 0, 0, tiled=True)  39.5 us
    ppermute x15, waiting for transfers between devices, ring(): return lax.ppermute(value, 'z', [(i, (i + step) % NZ) for i in range(NZ)])  33.2 us
    all_to_all x2, waiting for transfers between devices, exchange(): return lax.all_to_all(value, axes, 0, 0, tiled=True)  30.5 us
    ppermute x15, starting transfers between devices, ring(): return lax.ppermute(value, 'z', [(i, (i + step) % NZ) for i in range(NZ)])  20.9 us
    all_to_all x4, starting transfers between devices, spread(): return lax.all_to_all(copies, axes, 0, 0, tiled=True)  18.8 us
    all_to_all x2, starting transfers between devices, exchange(): return lax.all_to_all(value, axes, 0, 0, tiled=True)  13.7 us
    dot_general x2, matrix products, summed_logits(): part = jnp.dot(block, weight, preferred_element_type=F32).astype(F16)  11.4 us
    dot_general x1, matrix products, per_device(): lax.dot_general(jnp.concatenate([block, block_got]), jnp.concatenate([gra...  9.51 us
  transfers between devices with their start and end apart: 29, of which 16 were waited for; matrix products, arithmetic and copies ran while one was open for 27% of the time, Pallas kernels for 3%

profile of v2, /device:TPU:0, one launch (start us, length us, event | category | flops | bytes accessed | tf_op | source)
XLA Modules:
  0.0 239.6 jit_solution(1600567647444086850)
XLA Ops:
  2.3 1.6 broadcast_in_dim.48
  3.9 7.7 %all-to-all-start = ((bf16[32,128,256]{2,1,0:T(8,128)(2,1)}), bf16[32,128,256]{2,1,0:T(8,128)(2,1)S(1)}, u32[]{:S(2)}, u32[]{:S(2)}) async-start(bf16[32,128,256]{2,1,0:T(8,128)(2,1)} %bitcast.144), calls=%async_computation | async-start | bytes 4194304 | tf_op jit(solution)/shard_map/all_to_all | solution.py:30
  11.9 1.8 reshape.204
  13.8 3.2 %constant_dynamic-slice_fusion.22 = (bf16[1,1024,4,64]{1,0,3,2:T(2,128)(2,1)}, bf16[1,1024,4,64]{1,0,3,2:T(2,128)(2,1)S(1)}) fusion(bf16[2,1024,4,64]{1,0,3,2:T(2,128)(2,1)S(1)} %reshape.204, s32[]{:T(128)S(6)} %select_n.190, s32[]{:T(128)S(6)} %select_n.191), kind=kLoop, calls=%fused_computation.90 | loop fusion | bytes 2097160 | tf_op jit(solution)/shard_map/jit(dynamic_index_in_dim)/dynamic_slice | solution.py:39
  18.9 21.6 %all-to-all-done = bf16[32,128,256]{2,1,0:T(8,128)(2,1)S(1)} async-done(((bf16[32,128,256]{2,1,0:T(8,128)(2,1)}), bf16[32,128,256]{2,1,0:T(8,128)(2,1)S(1)}, u32[]{:S(2)}, u32[]{:S(2)}) %all-to-all-start) | async-done | bytes 2097184 | tf_op jit(solution)/shard_map/all_to_all | solution.py:30
  40.5 1.3 copy-done
  41.8 7.6 %attend.1 = bf16[32,1024]{1,0:T(8,128)(2,1)} custom-call(s32[64]{0:T(128)} %span_ref.1, s32[1]{0:T(128)} %bitcast.place_ref, bf16[32,1024]{1,0:T(8,128)(2,1)} %pad_maximum_fusion.4.query_ref, bf16[4096,256]{1,0:T(8,128)(2,1)} %bitcast.143), custom_call_target="tpu_custom_call" | custom-call | tf_op jit(solution)/shard_map/attend/pallas_call | solution.py:118
  49.4 2.0 broadcast_in_dim.82
  51.4 3.7 %all-to-all-start.1 = ((bf16[16,32,1024]{2,1,0:T(8,128)(2,1)}), bf16[16,32,1024]{2,1,0:T(8,128)(2,1)S(1)}, u32[]{:S(2)}, u32[]{:S(2)}) async-start(bf16[16,32,1024]{2,1,0:T(8,128)(2,1)} %broadcast_in_dim.82), calls=%async_computation.1 | async-start | bytes 2097152 | tf_op jit(solution)/shard_map/all_to_all | solution.py:35
  55.1 1.1 broadcast_in_dim.88
  56.2 1.6 copy.50
  58.1 1.2 fusion.7
  59.4 1.2 copy.49
  60.6 12.4 %all-to-all-done.1 = bf16[16,32,1024]{2,1,0:T(8,128)(2,1)S(1)} async-done(((bf16[16,32,1024]{2,1,0:T(8,128)(2,1)}), bf16[16,32,1024]{2,1,0:T(8,128)(2,1)S(1)}, u32[]{:S(2)}, u32[]{:S(2)}) %all-to-all-start.1) | async-done | bytes 1048608 | tf_op jit(solution)/shard_map/all_to_all | solution.py:35
  73.0 2.0 convolution_add_fusion.1
  75.6 1.4 collective-permute-done.2
  77.7 4.1 %collective-permute-start.5 = (f32[256,128]{1,0:T(8,128)S(1)}, f32[256,128]{1,0:T(8,128)S(1)}, u32[]{:S(2)}, u32[]{:S(2)}) collective-permute-start(f32[256,128]{1,0:T(8,128)S(1)} %bitcast.169), channel_id=1, source_target_pairs={{0,3},{1,0},{2,1},{3,2},{4,7},{5,4},{6,5},{7,6},{8,11},{9,8},{10,9... | collective-permute-start | bytes 393224 | tf_op jit(solution)/shard_map/ppermute | solution.py:43
  81.8 1.9 collective-permute-start.4
  83.7 1.2 collective-permute-done.5
  84.9 6.2 %collective-permute-done.3 = f32[256,128]{1,0:T(8,128)S(1)} collective-permute-done((f32[256,128]{1,0:T(8,128)S(1)}, f32[256,128]{1,0:T(8,128)S(1)}, u32[]{:S(2)}, u32[]{:S(2)}) %collective-permute-start.3) | collective-permute-done | bytes 131104 | tf_op jit(solution)/shard_map/ppermute | solution.py:43
  91.9 4.6 %all-to-all-start.2 = ((f32[64,2,128]{2,1,0:T(2,128)}), f32[64,2,128]{2,1,0:T(2,128)S(1)}, u32[]{:S(2)}, u32[]{:S(2)}) async-start(f32[64,2,128]{2,1,0:T(2,128)} %broadcast_in_dim.92), calls=%async_computation.2 | async-start | bytes 131072 | tf_op jit(solution)/shard_map/all_to_all | solution.py:35
  96.6 9.5 %all-to-all-done.2 = f32[64,2,128]{2,1,0:T(2,128)S(1)} async-done(((f32[64,2,128]{2,1,0:T(2,128)}), f32[64,2,128]{2,1,0:T(2,128)S(1)}, u32[]{:S(2)}, u32[]{:S(2)}) %all-to-all-start.2) | async-done | bytes 65568 | tf_op jit(solution)/shard_map/all_to_all | solution.py:35
  106.3 1.2 broadcast_in_dim.93
  107.5 3.8 %all-to-all-start.3 = ((bf16[16,256,128]{2,1,0:T(8,128)(2,1)}), bf16[16,256,128]{2,1,0:T(8,128)(2,1)S(1)}, u32[]{:S(2)}, u32[]{:S(2)}) async-start(bf16[16,256,128]{2,1,0:T(8,128)(2,1)} %broadcast_in_dim.93), calls=%async_computation.3 | async-start | bytes 2097152 | tf_op jit(solution)/shard_map/all_to_all | solution.py:35
  112.4 14.6 %all-to-all-done.3 = bf16[16,256,128]{2,1,0:T(8,128)(2,1)S(1)} async-done(((bf16[16,256,128]{2,1,0:T(8,128)(2,1)}), bf16[16,256,128]{2,1,0:T(8,128)(2,1)S(1)}, u32[]{:S(2)}, u32[]{:S(2)}) %all-to-all-start.3) | async-done | bytes 1048608 | tf_op jit(solution)/shard_map/all_to_all | solution.py:35
  127.9 5.7 %convolution_convert_fusion.2 = f16[256,2048]{1,0:T(8,128)(2,1)S(1)} fusion(bf16[2048,2048]{1,0:T(8,128)(2,1)} %param.17, bf16[32,8,16,128]{3,2,1,0:T(8,128)(2,1)S(1)} %bitcast.150), kind=kOutput, calls=%fused_computation.4 | convolution fusion | flops 2148007936 | bytes 10485760 | tf_op jit(solution)/shard_map/dot_general | solution.py:216
  133.8 1.3 collective-permute-start.9
  135.1 1.5 collective-permute-start.8
  136.6 5.7 %convolution_convert_fusion.1 = f16[256,2048]{1,0:T(8,128)(2,1)S(1)} fusion(bf16[2048,2048]{1,0:T(8,128)(2,1)} %collective-permute-done.10, bf16[32,8,16,128]{3,2,1,0:T(8,128)(2,1)S(1)} %bitcast.151), kind=kOutput, calls=%fused_computation.3 | convolution fusion | flops 2148007936 | bytes 10485760 | tf_op jit(solution)/shard_map/dot_general | solution.py:216
  142.4 3.3 %collective-permute-start.13 = (f16[64,2048]{1,0:T(8,128)(2,1)S(1)}, f16[64,2048]{1,0:T(8,128)(2,1)S(1)}, u32[]{:S(2)}, u32[]{:S(2)}) collective-permute-start(f16[64,2048]{1,0:T(8,128)(2,1)S(1)} %get-tuple-element.26), channel_id=1, source_target_pairs={{0,3},{1,0},{2,1},{3,2},{4,7},{5,4},{6,5},{7,6},{8,11},{9,8},{10,9... | collective-permute-start | bytes 786440 | tf_op jit(solution)/shard_map/ppermute | solution.py:43
  147.4 4.7 %collective-permute-done.7 = f16[64,2048]{1,0:T(8,128)(2,1)S(1)} collective-permute-done((f16[64,2048]{1,0:T(8,128)(2,1)S(1)}, f16[64,2048]{1,0:T(8,128)(2,1)S(1)}, u32[]{:S(2)}, u32[]{:S(2)}) %collective-permute-start.7) | collective-permute-done | bytes 262176 | tf_op jit(solution)/shard_map/ppermute | solution.py:43
  152.6 3.3 %collective-permute-done.13 = f16[64,2048]{1,0:T(8,128)(2,1)S(1)} collective-permute-done((f16[64,2048]{1,0:T(8,128)(2,1)S(1)}, f16[64,2048]{1,0:T(8,128)(2,1)S(1)}, u32[]{:S(2)}, u32[]{:S(2)}) %collective-permute-start.13) | collective-permute-done | bytes 262176 | tf_op jit(solution)/shard_map/ppermute | solution.py:43
  155.9 2.7 %collective-permute-done.11 = f16[64,2048]{1,0:T(8,128)(2,1)S(1)} collective-permute-done((f16[64,2048]{1,0:T(8,128)(2,1)S(1)}, f16[64,2048]{1,0:T(8,128)(2,1)S(1)}, u32[]{:S(2)}, u32[]{:S(2)}) %collective-permute-start.11) | collective-permute-done | bytes 262176 | tf_op jit(solution)/shard_map/ppermute | solution.py:43
  159.9 6.7 %all-to-all-start.4 = ((f32[64,8,128]{2,1,0:T(8,128)}), f32[64,8,128]{2,1,0:T(8,128)S(1)}, u32[]{:S(2)}, u32[]{:S(2)}) async-start(f32[64,8,128]{2,1,0:T(8,128)} %broadcast_in_dim.95), calls=%async_computation.4 | async-start | bytes 524288 | tf_op jit(solution)/shard_map/all_to_all | solution.py:35
  166.9 1.6 collective-permute-start.17
  168.5 2.7 %collective-permute-start.16 = (bf16[64,2048]{1,0:T(8,128)(2,1)S(1)}, bf16[64,2048]{1,0:T(8,128)(2,1)S(1)}, u32[]{:S(2)}, u32[]{:S(2)}) collective-permute-start(bf16[64,2048]{1,0:T(8,128)(2,1)S(1)} %get-tuple-element.38), channel_id=1, source_target_pairs={{0,2},{1,3},{2,0},{3,1},{4,6},{5,7},{6,4},{7,5},{8,10},{9,11},{10,... | collective-permute-start | bytes 786440 | tf_op jit(solution)/shard_map/ppermute | solution.py:43
  171.2 1.5 collective-permute-start.15
  174.1 3.0 %all-to-all-done.4 = f32[64,8,128]{2,1,0:T(8,128)S(1)} async-done(((f32[64,8,128]{2,1,0:T(8,128)}), f32[64,8,128]{2,1,0:T(8,128)S(1)}, u32[]{:S(2)}, u32[]{:S(2)}) %all-to-all-start.4) | async-done | bytes 262176 | tf_op jit(solution)/shard_map/all_to_all | solution.py:35
  178.0 6.7 %collective-permute-done.17 = bf16[64,2048]{1,0:T(8,128)(2,1)S(1)} collective-permute-done((bf16[64,2048]{1,0:T(8,128)(2,1)S(1)}, bf16[64,2048]{1,0:T(8,128)(2,1)S(1)}, u32[]{:S(2)}, u32[]{:S(2)}) %collective-permute-start.17) | collective-permute-done | bytes 262176 | tf_op jit(solution)/shard_map/ppermute | solution.py:43
  184.7 1.3 collective-permute-done.14
  187.8 2.7 %collective-permute-done.20 = bf16[64,2048]{1,0:T(8,128)(2,1)S(1)} collective-permute-done((bf16[64,2048]{1,0:T(8,128)(2,1)S(1)}, bf16[64,2048]{1,0:T(8,128)(2,1)S(1)}, u32[]{:S(2)}, u32[]{:S(2)}) %collective-permute-start.20) | collective-permute-done | bytes 262176 | tf_op jit(solution)/shard_map/ppermute | solution.py:43
  190.4 5.8 %collective-permute-done.19 = bf16[64,2048]{1,0:T(8,128)(2,1)S(1)} collective-permute-done((bf16[64,2048]{1,0:T(8,128)(2,1)S(1)}, bf16[64,2048]{1,0:T(8,128)(2,1)S(1)}, u32[]{:S(2)}, u32[]{:S(2)}) %collective-permute-start.19) | collective-permute-done | bytes 262176 | tf_op jit(solution)/shard_map/ppermute | solution.py:43
  196.2 3.5 %subtract_convert_fusion = (bf16[256,2048]{1,0:T(8,128)(2,1)}, bf16[256,2048]{1,0:T(8,128)(2,1)S(1)}) fusion(bf16[64,2048]{1,0:T(8,128)(2,1)S(1)} %collective-permute-done.20, bf16[64,2048]{1,0:T(8,128)(2,1)S(1)} %collective-permute-done.19, bf16[64,2048]{1,0:T(8,128)(2,1)S(1)} %collective-permute-done.18, bf16[64,2048]{1,0:T(8,128)(2,1)S(1)} %get-tuple-element.37, ...), kind=kLoop, calls=%fused_computation.11 | loop fusion | flops 13631488 | bytes 4213760 | tf_op jit(solution)/shard_map/convert_element_type | solution.py:252
  199.7 6.1 %fusion.38 = f32[256,2048]{1,0:T(8,128)S(1)} fusion(bf16[256,2048]{1,0:T(8,128)(2,1)S(1)} %get-tuple-element.64, bf16[2048,2048]{1,0:T(8,128)(2,1)} %param.17), kind=kOutput, calls=%fused_computation.126 | convolution fusion | flops 2147483648 | bytes 11534336 | tf_op jit(solution)/shard_map/dot_general | solution.py:259
  205.9 6.1 %fusion = bf16[256,2048]{1,0:T(8,128)(2,1)S(1)} fusion(f32[256,2048]{1,0:T(8,128)S(1)} %fusion.38, bf16[256,2048]{1,0:T(8,128)(2,1)} %get-tuple-element.63, bf16[2048,2048]{1,0:T(8,128)(2,1)} %collective-permute-done.10), kind=kOutput, calls=%fused_computation.2 | convolution fusion | flops 2148532224 | bytes 12582912 | tf_op jit(solution)/shard_map/dot_general | solution.py:261
  213.2 6.0 %all-to-all-start.5 = ((bf16[16,16,2048]{2,1,0:T(8,128)(2,1)}), bf16[16,16,2048]{2,1,0:T(8,128)(2,1)S(1)}, u32[]{:S(2)}, u32[]{:S(2)}) async-start(bf16[16,16,2048]{2,1,0:T(8,128)(2,1)} %bitcast.57), calls=%async_computation.5 | async-start | bytes 2097152 | tf_op jit(solution)/shard_map/all_to_all | solution.py:30
  219.3 9.5 %convolution_convert_fusion = bf16[2048,2048]{1,0:T(8,128)(2,1)} fusion(bf16[256,2048]{1,0:T(8,128)(2,1)} %collective-permute-done.21, bf16[256,2048]{1,0:T(8,128)(2,1)S(1)} %bitcast.161, bf16[256,2048]{1,0:T(8,128)(2,1)} %collective-permute-done.22, bf16[256,2048]{1,0:T(8,128)(2,1)S(1)} %copy-done.3), kind=kOutput, calls=%fused_computation | convolution fusion | flops 4307550208 | bytes 12582912 | tf_op jit(solution)/shard_map/dot_general | solution.py:264
  228.8 8.9 %all-to-all-done.5 = bf16[16,16,2048]{2,1,0:T(8,128)(2,1)S(1)} async-done(((bf16[16,16,2048]{2,1,0:T(8,128)(2,1)}), bf16[16,16,2048]{2,1,0:T(8,128)(2,1)S(1)}, u32[]{:S(2)}, u32[]{:S(2)}) %all-to-all-start.5) | async-done | bytes 1048608 | tf_op jit(solution)/shard_map/all_to_all | solution.py:30
  (108 shorter events, 17.5 us)
Async XLA Ops:
  0.6 135.9 %collective-permute-start.10 = (bf16[2048,2048]{1,0:T(8,128)(2,1)}, bf16[2048,2048]{1,0:T(8,128)(2,1)}, u32[]{:S(2)}, u32[]{:S(2)}) collective-permute-start(bf16[2048,2048]{1,0:T(8,128)(2,1)} %param.17), channel_id=1, source_target_pairs={{0,4},{4,0},{1,5},{5,1},{2,6},{6,2},{3,7},{7,3},{8,12},{12,8},{9,1... | collective-permute-start | bytes 25165832 | tf_op jit(solution)/shard_map/ppermute | solution.py:26
  3.9 7.7 %copy-start.4 = (bf16[16,2048]{1,0:T(8,128)(2,1)S(1)}, bf16[16,2048]{1,0:T(8,128)(2,1)}, u32[]{:S(2)}) copy-start(bf16[16,2048]{1,0:T(8,128)(2,1)} %param.9) | copy-start | bytes 196612
  3.9 36.6 %all-to-all-start = ((bf16[32,128,256]{2,1,0:T(8,128)(2,1)}), bf16[32,128,256]{2,1,0:T(8,128)(2,1)S(1)}, u32[]{:S(2)}, u32[]{:S(2)}) async-start(bf16[32,128,256]{2,1,0:T(8,128)(2,1)} %bitcast.144), calls=%async_computation | async-start | bytes 4194304 | tf_op jit(solution)/shard_map/all_to_all | solution.py:30
  11.6 6.6 %collective-permute-start = (bf16[16,1024]{1,0:T(8,128)(2,1)S(1)}, bf16[16,1024]{1,0:T(8,128)(2,1)S(1)}, u32[]{:S(2)}, u32[]{:S(2)}) collective-permute-start(bf16[16,1024]{1,0:T(8,128)(2,1)S(1)} %broadcast_select_fusion.2), channel_id=1, source_target_pairs={{0,4},{4,0},{1,5},{5,1},{2,6},{6,2},{3,7},{7,3},{8,12},{12,8},{9,1... | collective-permute-start | bytes 98312 | tf_op jit(solution)/shard_map/ppermute | solution.py:26
  18.0 40.1 %collective-permute-start.1 = (bf16[1024,4,64]{0,2,1:T(8,128)(2,1)}, bf16[1024,4,64]{0,2,1:T(8,128)(2,1)}, u32[]{:S(2)}, u32[]{:S(2)}) collective-permute-start(bf16[1024,4,64]{0,2,1:T(8,128)(2,1)} %bitcast.136), channel_id=1, source_target_pairs={{0,4},{4,0},{1,5},{5,1},{2,6},{6,2},{3,7},{7,3},{8,12},{12,8},{9,1... | collective-permute-start | bytes 1572872 | tf_op jit(solution)/shard_map/ppermute | solution.py:26
  40.5 1.3 copy-start
  49.4 5.6 %copy-start.5 = (bf16[512,1,1,64]{0,3,2,1:T(8,128)(2,1)S(1)}, bf16[512,1,1,64]{0,3,2,1:T(8,128)(2,1)}, u32[]{:S(2)}) copy-start(bf16[512,1,1,64]{0,3,2,1:T(8,128)(2,1)} %param.15) | copy-start | bytes 196612
  51.4 21.6 %all-to-all-start.1 = ((bf16[16,32,1024]{2,1,0:T(8,128)(2,1)}), bf16[16,32,1024]{2,1,0:T(8,128)(2,1)S(1)}, u32[]{:S(2)}, u32[]{:S(2)}) async-start(bf16[16,32,1024]{2,1,0:T(8,128)(2,1)} %broadcast_in_dim.82), calls=%async_computation.1 | async-start | bytes 2097152 | tf_op jit(solution)/shard_map/all_to_all | solution.py:35
  55.1 3.0 %copy-start.1 = (bf16[1,1024,4,64]{1,0,3,2:T(2,128)(2,1)S(1)}, bf16[1,1024,4,64]{1,0,3,2:T(2,128)(2,1)}, u32[]{:S(2)}) copy-start(bf16[1,1024,4,64]{1,0,3,2:T(2,128)(2,1)} %get-tuple-element.35) | copy-start | bytes 1572868
  72.9 2.1 copy-start.7
  75.0 2.0 collective-permute-start.2
  75.1 8.6 %collective-permute-start.6 = (f32[64]{0:T(128)S(1)}, f32[64]{0:T(128)S(1)}, u32[]{:S(2)}, u32[]{:S(2)}) collective-permute-start(f32[64]{0:T(128)S(1)} %bitcast.178), channel_id=1, source_target_pairs={{0,4},{4,0},{1,5},{5,1},{2,6},{6,2},{3,7},{7,3},{8,12},{12,8},{9,1... | collective-permute-start | bytes 776 | tf_op jit(solution)/shard_map/ppermute | solution.py:26
  77.7 7.2 %collective-permute-start.5 = (f32[256,128]{1,0:T(8,128)S(1)}, f32[256,128]{1,0:T(8,128)S(1)}, u32[]{:S(2)}, u32[]{:S(2)}) collective-permute-start(f32[256,128]{1,0:T(8,128)S(1)} %bitcast.169), channel_id=1, source_target_pairs={{0,3},{1,0},{2,1},{3,2},{4,7},{5,4},{6,5},{7,6},{8,11},{9,8},{10,9... | collective-permute-start | bytes 393224 | tf_op jit(solution)/shard_map/ppermute | solution.py:43
  81.8 9.3 %collective-permute-start.3 = (f32[256,128]{1,0:T(8,128)S(1)}, f32[256,128]{1,0:T(8,128)S(1)}, u32[]{:S(2)}, u32[]{:S(2)}) collective-permute-start(f32[256,128]{1,0:T(8,128)S(1)} %bitcast.168), channel_id=1, source_target_pairs={{0,1},{1,2},{2,3},{3,0},{4,5},{5,6},{6,7},{7,4},{8,9},{9,10},{10,1... | collective-permute-start | bytes 393224 | tf_op jit(solution)/shard_map/ppermute | solution.py:43
  81.8 9.3 %collective-permute-start.4 = (f32[256,128]{1,0:T(8,128)S(1)}, f32[256,128]{1,0:T(8,128)S(1)}, u32[]{:S(2)}, u32[]{:S(2)}) collective-permute-start(f32[256,128]{1,0:T(8,128)S(1)} %bitcast.167), channel_id=1, source_target_pairs={{0,2},{1,3},{2,0},{3,1},{4,6},{5,7},{6,4},{7,5},{8,10},{9,11},{10,... | collective-permute-start | bytes 393224 | tf_op jit(solution)/shard_map/ppermute | solution.py:43
  91.1 20.2 %copy-start.6 = (s32[512]{0:T(512)S(1)}, s32[512]{0:T(512)}, u32[]{:S(2)}) copy-start(s32[512]{0:T(512)} %param.13) | copy-start | bytes 6148
  91.9 14.2 %all-to-all-start.2 = ((f32[64,2,128]{2,1,0:T(2,128)}), f32[64,2,128]{2,1,0:T(2,128)S(1)}, u32[]{:S(2)}, u32[]{:S(2)}) async-start(f32[64,2,128]{2,1,0:T(2,128)} %broadcast_in_dim.92), calls=%async_computation.2 | async-start | bytes 131072 | tf_op jit(solution)/shard_map/all_to_all | solution.py:35
  107.5 19.5 %all-to-all-start.3 = ((bf16[16,256,128]{2,1,0:T(8,128)(2,1)}), bf16[16,256,128]{2,1,0:T(8,128)(2,1)S(1)}, u32[]{:S(2)}, u32[]{:S(2)}) async-start(bf16[16,256,128]{2,1,0:T(8,128)(2,1)} %broadcast_in_dim.93), calls=%async_computation.3 | async-start | bytes 2097152 | tf_op jit(solution)/shard_map/all_to_all | solution.py:35
  133.8 12.8 %collective-permute-start.9 = (f16[64,2048]{1,0:T(8,128)(2,1)S(1)}, f16[64,2048]{1,0:T(8,128)(2,1)S(1)}, u32[]{:S(2)}, u32[]{:S(2)}) collective-permute-start(f16[64,2048]{1,0:T(8,128)(2,1)S(1)} %get-tuple-element.29), channel_id=1, source_target_pairs={{0,3},{1,0},{2,1},{3,2},{4,7},{5,4},{6,5},{7,6},{8,11},{9,8},{10,9... | collective-permute-start | bytes 786440 | tf_op jit(solution)/shard_map/ppermute | solution.py:43
  135.1 12.3 %collective-permute-start.8 = (f16[64,2048]{1,0:T(8,128)(2,1)S(1)}, f16[64,2048]{1,0:T(8,128)(2,1)S(1)}, u32[]{:S(2)}, u32[]{:S(2)}) collective-permute-start(f16[64,2048]{1,0:T(8,128)(2,1)S(1)} %get-tuple-element.30), channel_id=1, source_target_pairs={{0,2},{1,3},{2,0},{3,1},{4,6},{5,7},{6,4},{7,5},{8,10},{9,11},{10,... | collective-permute-start | bytes 786440 | tf_op jit(solution)/shard_map/ppermute | solution.py:43
  136.5 15.5 %collective-permute-start.7 = (f16[64,2048]{1,0:T(8,128)(2,1)S(1)}, f16[64,2048]{1,0:T(8,128)(2,1)S(1)}, u32[]{:S(2)}, u32[]{:S(2)}) collective-permute-start(f16[64,2048]{1,0:T(8,128)(2,1)S(1)} %get-tuple-element.28), channel_id=1, source_target_pairs={{0,1},{1,2},{2,3},{3,0},{4,5},{5,6},{6,7},{7,4},{8,9},{9,10},{10,1... | collective-permute-start | bytes 786440 | tf_op jit(solution)/shard_map/ppermute | solution.py:43
  142.4 13.5 %collective-permute-start.13 = (f16[64,2048]{1,0:T(8,128)(2,1)S(1)}, f16[64,2048]{1,0:T(8,128)(2,1)S(1)}, u32[]{:S(2)}, u32[]{:S(2)}) collective-permute-start(f16[64,2048]{1,0:T(8,128)(2,1)S(1)} %get-tuple-element.26), channel_id=1, source_target_pairs={{0,3},{1,0},{2,1},{3,2},{4,7},{5,4},{6,5},{7,6},{8,11},{9,8},{10,9... | collective-permute-start | bytes 786440 | tf_op jit(solution)/shard_map/ppermute | solution.py:43
  145.7 10.2 %collective-permute-start.12 = (f16[64,2048]{1,0:T(8,128)(2,1)S(1)}, f16[64,2048]{1,0:T(8,128)(2,1)S(1)}, u32[]{:S(2)}, u32[]{:S(2)}) collective-permute-start(f16[64,2048]{1,0:T(8,128)(2,1)S(1)} %get-tuple-element.27), channel_id=1, source_target_pairs={{0,2},{1,3},{2,0},{3,1},{4,6},{5,7},{6,4},{7,5},{8,10},{9,11},{10,... | collective-permute-start | bytes 786440 | tf_op jit(solution)/shard_map/ppermute | solution.py:43
  146.6 12.0 %collective-permute-start.11 = (f16[64,2048]{1,0:T(8,128)(2,1)S(1)}, f16[64,2048]{1,0:T(8,128)(2,1)S(1)}, u32[]{:S(2)}, u32[]{:S(2)}) collective-permute-start(f16[64,2048]{1,0:T(8,128)(2,1)S(1)} %get-tuple-element.25), channel_id=1, source_target_pairs={{0,1},{1,2},{2,3},{3,0},{4,5},{5,6},{6,7},{7,4},{8,9},{9,10},{10,1... | collective-permute-start | bytes 786440 | tf_op jit(solution)/shard_map/ppermute | solution.py:43
  159.9 17.3 %all-to-all-start.4 = ((f32[64,8,128]{2,1,0:T(8,128)}), f32[64,8,128]{2,1,0:T(8,128)S(1)}, u32[]{:S(2)}, u32[]{:S(2)}) async-start(f32[64,8,128]{2,1,0:T(8,128)} %broadcast_in_dim.95), calls=%async_computation.4 | async-start | bytes 524288 | tf_op jit(solution)/shard_map/all_to_all | solution.py:35
  166.9 17.8 %collective-permute-start.17 = (bf16[64,2048]{1,0:T(8,128)(2,1)S(1)}, bf16[64,2048]{1,0:T(8,128)(2,1)S(1)}, u32[]{:S(2)}, u32[]{:S(2)}) collective-permute-start(bf16[64,2048]{1,0:T(8,128)(2,1)S(1)} %get-tuple-element.38), channel_id=1, source_target_pairs={{0,1},{1,2},{2,3},{3,0},{4,5},{5,6},{6,7},{7,4},{8,9},{9,10},{10,1... | collective-permute-start | bytes 786440 | tf_op jit(solution)/shard_map/ppermute | solution.py:43
  168.5 19.0 %collective-permute-start.16 = (bf16[64,2048]{1,0:T(8,128)(2,1)S(1)}, bf16[64,2048]{1,0:T(8,128)(2,1)S(1)}, u32[]{:S(2)}, u32[]{:S(2)}) collective-permute-start(bf16[64,2048]{1,0:T(8,128)(2,1)S(1)} %get-tuple-element.38), channel_id=1, source_target_pairs={{0,2},{1,3},{2,0},{3,1},{4,6},{5,7},{6,4},{7,5},{8,10},{9,11},{10,... | collective-permute-start | bytes 786440 | tf_op jit(solution)/shard_map/ppermute | solution.py:43
  171.2 16.6 %collective-permute-start.15 = (bf16[64,2048]{1,0:T(8,128)(2,1)S(1)}, bf16[64,2048]{1,0:T(8,128)(2,1)S(1)}, u32[]{:S(2)}, u32[]{:S(2)}) collective-permute-start(bf16[64,2048]{1,0:T(8,128)(2,1)S(1)} %get-tuple-element.38), channel_id=1, source_target_pairs={{0,3},{1,0},{2,1},{3,2},{4,7},{5,4},{6,5},{7,6},{8,11},{9,8},{10,9... | collective-permute-start | bytes 786440 | tf_op jit(solution)/shard_map/ppermute | solution.py:43
  172.7 17.8 %collective-permute-start.20 = (bf16[64,2048]{1,0:T(8,128)(2,1)S(1)}, bf16[64,2048]{1,0:T(8,128)(2,1)S(1)}, u32[]{:S(2)}, u32[]{:S(2)}) collective-permute-start(bf16[64,2048]{1,0:T(8,128)(2,1)S(1)} %get-tuple-element.37), channel_id=1, source_target_pairs={{0,1},{1,2},{2,3},{3,0},{4,5},{5,6},{6,7},{7,4},{8,9},{9,10},{10,1... | collective-permute-start | bytes 786440 | tf_op jit(solution)/shard_map/ppermute | solution.py:43
  173.2 23.0 %collective-permute-start.19 = (bf16[64,2048]{1,0:T(8,128)(2,1)S(1)}, bf16[64,2048]{1,0:T(8,128)(2,1)S(1)}, u32[]{:S(2)}, u32[]{:S(2)}) collective-permute-start(bf16[64,2048]{1,0:T(8,128)(2,1)S(1)} %get-tuple-element.37), channel_id=1, source_target_pairs={{0,2},{1,3},{2,0},{3,1},{4,6},{5,7},{6,4},{7,5},{8,10},{9,11},{10,... | collective-permute-start | bytes 786440 | tf_op jit(solution)/shard_map/ppermute | solution.py:43
  184.7 1.3 collective-permute-start.14
  186.0 10.2 %collective-permute-start.18 = (bf16[64,2048]{1,0:T(8,128)(2,1)S(1)}, bf16[64,2048]{1,0:T(8,128)(2,1)S(1)}, u32[]{:S(2)}, u32[]{:S(2)}) collective-permute-start(bf16[64,2048]{1,0:T(8,128)(2,1)S(1)} %get-tuple-element.37), channel_id=1, source_target_pairs={{0,3},{1,0},{2,1},{3,2},{4,7},{5,4},{6,5},{7,6},{8,11},{9,8},{10,9... | collective-permute-start | bytes 786440 | tf_op jit(solution)/shard_map/ppermute | solution.py:43
  187.5 31.8 %collective-permute-start.21 = (bf16[256,2048]{1,0:T(8,128)(2,1)S(1)}, bf16[256,2048]{1,0:T(8,128)(2,1)}, u32[]{:S(2)}, u32[]{:S(2)}) collective-permute-start(bf16[256,2048]{1,0:T(8,128)(2,1)S(1)} %bitcast.160), channel_id=1, source_target_pairs={{0,4},{4,0},{1,5},{5,1},{2,6},{6,2},{3,7},{7,3},{8,12},{12,8},{9,1... | collective-permute-start | bytes 3145736 | tf_op jit(solution)/shard_map/ppermute | solution.py:26
  199.7 6.1 %copy-start.2 = (bf16[256,2048]{1,0:T(8,128)(2,1)}, bf16[256,2048]{1,0:T(8,128)(2,1)S(1)}, u32[]{:S(2)}) copy-start(bf16[256,2048]{1,0:T(8,128)(2,1)S(1)} %get-tuple-element.64) | copy-start | bytes 3145732
  205.8 13.5 %collective-permute-start.22 = (bf16[256,2048]{1,0:T(8,128)(2,1)}, bf16[256,2048]{1,0:T(8,128)(2,1)}, u32[]{:S(2)}, u32[]{:S(2)}) collective-permute-start(bf16[256,2048]{1,0:T(8,128)(2,1)} %get-tuple-element.63), channel_id=1, source_target_pairs={{0,4},{4,0},{1,5},{5,1},{2,6},{6,2},{3,7},{7,3},{8,12},{12,8},{9,1... | collective-permute-start | bytes 3145736 | tf_op jit(solution)/shard_map/ppermute | solution.py:26
  212.1 7.2 %copy-start.3 = (bf16[256,2048]{1,0:T(8,128)(2,1)S(1)}, bf16[256,2048]{1,0:T(8,128)(2,1)}, u32[]{:S(2)}) copy-start(bf16[256,2048]{1,0:T(8,128)(2,1)} %copy-done.2) | copy-start | bytes 3145732
  213.2 24.5 %all-to-all-start.5 = ((bf16[16,16,2048]{2,1,0:T(8,128)(2,1)}), bf16[16,16,2048]{2,1,0:T(8,128)(2,1)S(1)}, u32[]{:S(2)}, u32[]{:S(2)}) async-start(bf16[16,16,2048]{2,1,0:T(8,128)(2,1)} %bitcast.57), calls=%async_computation.5 | async-start | bytes 2097152 | tf_op jit(solution)/shard_map/all_to_all | solution.py:30
